TPU v7x, 32 devices: a whole 2x2x4 slice. The times are simulated.
32 devices in a mesh: wide: 8 (over z, x), narrow: 4 (over y, core).
Axes of the slice: x: 2, y: 2, z: 4, core: 2. Of those that a mesh axis runs over, the one named last changes fastest.
Arguments:
- tokens: bfloat16 [64, 512, 768], P(('wide', 'narrow')), may hold values from -6 to 6
- doc_lengths: int32 [64], P(('wide', 'narrow')), may hold values from 30 to 512
- qkv_weight: bfloat16 [768, 2304], replicated, may hold values from -0.21875 to 0.21875
- query_bias: bfloat16 [768], replicated, may hold values from -3 to 3
- value_bias: bfloat16 [768], replicated, may hold values from -3 to 3
- out_weight: bfloat16 [768, 768], replicated, may hold values from -0.625 to 0.625
- out_bias: bfloat16 [768], replicated, may hold values from -1.75 to 1.75
- first_gain: bfloat16 [768], replicated, may hold values from 0.5 to 1.5
- first_shift: bfloat16 [768], replicated, may hold values from -1.75 to 1.75
- up_weight: bfloat16 [768, 3072], replicated, may hold values from -0.21875 to 0.21875
- up_bias: bfloat16 [3072], replicated, may hold values from -3 to 3
- down_weight: bfloat16 [3072, 768], replicated, may hold values from -0.15625 to 0.15625
- down_bias: bfloat16 [768], replicated, may hold values from -1.75 to 1.75
- second_gain: bfloat16 [768], replicated, may hold values from 0.5 to 1.5
- second_shift: bfloat16 [768], replicated, may hold values from -1.75 to 1.75
- dir_weight: bfloat16 [1536, 8], replicated, may hold values from -0.375 to 0.375
- dir_bias: bfloat16 [8], replicated, may hold values from -1 to 1
- segment_rows: int32 [64, 128], P(('wide', 'narrow')), may hold values from 0 to 511, as said below
- segment_slots: int32 [32, 256], P(('wide', 'narrow')), may hold values from 0 to 255, each once within a row
- pair_rows: int32 [32, 256, 2], P(('wide', 'narrow')), may hold values from 0 to 255
- pair_labels: int32 [32, 256], P(('wide', 'narrow')), may hold values from 0 to 7
- out_cotangent: bfloat16 [64, 512, 768], P(('wide', 'narrow')), may hold values from -6 to 6
Outputs:
- encoded: bfloat16 [64, 512, 768], P(('wide', 'narrow'))
- grad_tokens: bfloat16 [64, 512, 768], P(('wide', 'narrow'))
- grad_qkv_weight: float32 [768, 2304], P('narrow', 'wide')
- grad_query_bias: float32 [768], replicated
- grad_value_bias: float32 [768], replicated
- grad_out_weight: float32 [768, 768], P('narrow', 'wide')
- grad_out_bias: float32 [768], replicated
- grad_first_gain: float32 [768], replicated
- grad_first_shift: float32 [768], replicated
- grad_up_weight: float32 [768, 3072], P('narrow', 'wide')
- grad_up_bias: float32 [3072], replicated
- grad_down_weight: float32 [3072, 768], P('narrow', 'wide')
- grad_down_bias: float32 [768], replicated
- grad_second_gain: float32 [768], replicated
- grad_second_shift: float32 [768], replicated
- grad_dir_weight: float32 [1536, 8], replicated
- grad_dir_bias: float32 [8], replicated
Inputs may be any that keep to these rules, and one draw needn't show every extreme that they name: `segment_rows`: each value is below the token count of its document. `segment_slots`: each device's row holds every slot once.
All inputs are finite; a program needn't handle non-finite values.
Results may differ from a plain program's by a relative error of at most 0.02.
Values may be sent and summed in bfloat16 or wider, within the bound.
A program may use at most 192 MiB of HBM per device.

v0:
```python
import jax
import jax.numpy as jnp
from jax import lax
from jax.experimental import pallas as pl
from jax.experimental.pallas import tpu as pltpu
from jax.sharding import PartitionSpec as P

HEADS = 12
HEAD_DIM = 64


EXACT = lax.Precision.HIGHEST
MASKED = -1e30
EPSILON = 1e-05


def norm_forward(values, gain, shift):
    center = jnp.mean(values, -1, keepdims=True)
    centered = values - center
    inverse = lax.rsqrt(jnp.mean(centered * centered, -1, keepdims=True) + EPSILON)
    normed = centered * inverse
    return (normed * gain + shift, normed, inverse)


def norm_backward(grad, normed, inverse, gain):
    scaled = grad * gain
    first_mean = jnp.mean(scaled, -1, keepdims=True)
    second_mean = jnp.mean(scaled * normed, -1, keepdims=True)
    return (
        (scaled - first_mean - normed * second_mean) * inverse,
        jnp.sum(grad * normed, 0),
        jnp.sum(grad, 0),
    )


def normal_cdf(values):
    return 0.5 * (1.0 + lax.erf(values * 0.7071067811865476))


MESH_ID = pl.DeviceIdType.MESH


def axis_bits():
    names = []
    for axis in ("wide", "narrow"):
        count = lax.axis_size(axis).bit_length() - 1
        names += [(axis, bit) for bit in reversed(range(count))]
    return names


class Place:
    def __init__(self):
        self.index = {axis: lax.axis_index(axis) for axis in ("wide", "narrow")}
        self.names = axis_bits()
        self.bit = {name: (self.index[name[0]] // (1 << name[1])) % 2 for name in self.names}

    def across(self, name):
        axis, bit = name
        target = dict(self.index)
        target[axis] = target[axis] + (1 << bit) - (2 << bit) * self.bit[name]
        return target

    def ahead(self, offset):
        target = dict(self.index)
        target["wide"] = (target["wide"] + offset) % lax.axis_size("wide")
        return target

    def greet(self, all_wide=False):
        barrier = pltpu.get_barrier_semaphore()
        targets = [self.across(name) for name in self.names if not (all_wide and name[0] == "wide")]
        if all_wide:
            targets += [self.ahead(offset) for offset in range(1, lax.axis_size("wide"))]
        for target in targets:
            pl.semaphore_signal(barrier, inc=1, device_id=target, device_id_type=MESH_ID)
        pl.semaphore_wait(barrier, len(targets))


class Halving:
    def __init__(self, place, names, order, source, own, received, send_sems, recv_sems, first_sem):
        self.place, self.names, self.order = place, names, order
        self.source, self.own, self.received = source, own, received
        self.send_sems, self.recv_sems, self.first_sem = send_sems, recv_sems, first_sem

    def region(self, step, mine):
        index = []
        for name in self.names:
            if name in self.order[:step]:
                index.append(self.place.bit[name])
            elif name == self.order[step]:
                index.append(self.place.bit[name] if mine else 1 - self.place.bit[name])
            else:
                index.append(slice(None))
        return tuple(index)

    def copy(self, step):
        held = self.source if step == 0 else self.own
        return pltpu.make_async_remote_copy(
            src_ref=held.at[self.region(step, False)],
            dst_ref=self.received[step],
            send_sem=self.send_sems.at[self.first_sem + step],
            recv_sem=self.recv_sems.at[self.first_sem + step],
            device_id=self.place.across(self.order[step]),
            device_id_type=MESH_ID,
        )

    def send(self, step):
        self.copy(step).start()

    def add(self, step):
        self.copy(step).wait_recv()
        mine = self.region(step, True)
        if step + 1 < len(self.order):
            self.own[mine] = self.own[mine] + self.received[step][...]
            return None
        return self.own[mine].astype(jnp.float32) + self.received[step][...].astype(jnp.float32)

    def merge(self, step):
        self.copy(step).wait_recv()
        mine = self.region(step, True)
        self.own[mine] = self.own[mine] + self.received[step][...]

    def close(self):
        for step in range(len(self.order)):
            self.copy(step).wait_send()


def link_orders():
    wide = [("wide", bit) for bit in range(lax.axis_size("wide").bit_length() - 1)]
    narrow = [("narrow", bit) for bit in range(1, lax.axis_size("narrow").bit_length() - 1)]
    core, x, near, far = [("narrow", 0)], wide[:1], wide[1:-1], wide[-1:]
    return [core + narrow + x + near + far, core + x + near + narrow + far, core + near + narrow + x + far]


def attention_forward(qkv, key_bias, docs, length):
    width = qkv.shape[1] // 3
    pairs = width // 128

    def kernel(q_ref, k_ref, v_ref, bias_ref, mixed_ref, total_ref):
        lane = lax.broadcasted_iota(jnp.int32, (1, 128), 1)
        keys, values = k_ref[...], v_ref[...]
        queries = q_ref[...] * jnp.bfloat16(HEAD_DIM**-0.5)
        results = []
        for head in range(2):
            inside = (lane // HEAD_DIM) == head
            masked = jnp.where(inside, queries, jnp.zeros_like(queries))
            scores = dot_last(masked, keys) + bias_ref[0]
            highest = jnp.max(scores, -1, keepdims=True)
            powers = jnp.exp(scores - highest)
            summed = jnp.sum(powers, -1, keepdims=True)
            out = jnp.dot(powers.astype(jnp.bfloat16), values, preferred_element_type=jnp.float32)
            results.append((out / summed, highest + jnp.log(summed)))
        first = lane < HEAD_DIM
        mixed_ref[...] = jnp.where(first, results[0][0], results[1][0]).astype(jnp.bfloat16)
        total_ref[...] = jnp.where(first, results[0][1], results[1][1])

    def block(which):
        return pl.BlockSpec((length, 128), lambda doc, pair: (doc, which * pairs + pair))

    rows = docs * length
    return pl.pallas_call(
        kernel,
        grid=(docs, pairs),
        in_specs=[block(0), block(1), block(2), pl.BlockSpec((1, 1, length), lambda doc, pair: (doc, 0, 0))],
        out_specs=[block(0), block(0)],
        out_shape=[
            jax.ShapeDtypeStruct((rows, width), jnp.bfloat16),
            jax.ShapeDtypeStruct((rows, width), jnp.float32),
        ],
        compiler_params=pltpu.CompilerParams(vmem_limit_bytes=48 << 20),
        name="attention_forward",
    )(qkv, qkv, qkv, key_bias)


def dot_last(left, right):
    return lax.dot_general(left, right, (((1,), (1,)), ((), ())), preferred_element_type=jnp.float32)


def norm_back_rows(grad, normed, inverse, gain):
    scaled = grad * gain
    first = jnp.mean(scaled, -1, keepdims=True)
    second = jnp.mean(scaled * normed, -1, keepdims=True)
    return (scaled - first - normed * second) * inverse


def parts_of(values, count):
    terms = []
    for _ in range(count):
        term = values.astype(jnp.bfloat16).astype(jnp.float32)
        terms.append(term)
        values = values - term
    return jnp.concatenate(terms).astype(jnp.bfloat16)


def one_hot(row, count):
    lines = lax.broadcasted_iota(jnp.int32, (count, row.shape[1]), 0)
    return jnp.where(lines == row, 1.0, 0.0).astype(jnp.bfloat16)


def ffn_backward(lengths, numbers, encoded, cotangent, dir_rows, dir_bias, normed_two, inverse_two, second_gain, active, slope, hidden_low, down_weight, up_weight,
                 normed_one, inverse_one, first_gain):
    rows, width = hidden_low.shape
    ff = active.shape[1]
    segments, classes = numbers.shape[1], dir_bias.shape[0]
    length = rows // lengths.shape[0]
    names = axis_bits()
    steps = len(names)
    wide, narrow = lax.axis_size("wide"), lax.axis_size("narrow")
    wide_bits, narrow_bits = wide.bit_length() - 1, narrow.bit_length() - 1
    chunks = ff // narrow // 128
    third = chunks // 2
    d_rows, u_rows = width // wide, width // narrow
    row_block = 128
    row_steps = rows // row_block
    orders = link_orders()
    two = (2,)
    first_dir = 6 + narrow
    sum_rows = pl.cdiv(first_dir + 3 * classes, 8) * 8

    def chunk_of(step):
        step = jnp.clip(step, 0, chunks - 1)
        return step // 2 + third * (step % 2)

    def bits_of(number, count):
        return tuple((number >> bit) & 1 for bit in reversed(range(count)))

    def kernel(*refs):
        lens, nums, enc, cot, dir_w, dir_b = refs[:6]
        refs = refs[6:]
        (n2, q2, gain2, n1, q1, gain1, hidden) = refs[:7]
        refs = refs[7:]
        act = refs[:narrow]
        slo = refs[narrow : 2 * narrow]
        dws = refs[2 * narrow : 3 * narrow]
        uws = refs[3 * narrow : 4 * narrow]
        rest = list(refs[4 * narrow :])
        ga_out, up_out, down_out, sums_out = rest[:4]
        rest = rest[4:]
        grad_hidden, lowered, lowered_t, hidden_t, own, up_own, up_received = rest[:7]
        received = rest[7 : 7 + steps]
        select, leaving, arrived, leaving_grads, arrived_grads = rest[7 + steps : 12 + steps]
        send_sems, recv_sems, local_sems = rest[12 + steps :]
        pid = pl.program_id(0)
        place = Place()
        pieces = []
        for number in range(chunks):
            pieces.append(
                Halving(place, names, orders[number % 3], own.at[number], own.at[number],
                        [r.at[number] for r in received], send_sems, recv_sems, number * steps)
            )
        core = ("narrow", 0)
        up_names = [name for name in names if name != ("wide", 0)]
        up_pieces = [
            Halving(place, up_names, [core], up_own.at[number], up_own.at[number], [up_received.at[number]],
                    send_sems, recv_sems, chunks * steps + number)
            for number in range(chunks)
        ]

        def up_write(number):
            mine = up_pieces[number].region(0, True)
            return pltpu.make_async_copy(
                up_own.at[number].at[mine],
                up_out.at[(number // 2,) + (slice(None),) * (wide_bits - 1) + (number % 2,)],
                local_sems.at[number],
            )

        def exchange(source, landing, first):
            made = []
            for offset in range(1, wide):
                target = place.ahead(offset)
                made.append(pltpu.make_async_remote_copy(
                    src_ref=source.at[target["wide"]], dst_ref=landing.at[place.index["wide"]],
                    send_sem=send_sems.at[first + offset - 1], recv_sem=recv_sems.at[first + offset - 1],
                    device_id=target, device_id_type=MESH_ID))
            me = place.index["wide"]
            for copy in made:
                copy.start()
            landing[me] = source[me]
            for copy in made:
                copy.wait()
            return landing[...].reshape(segments, width)

        @pl.when(pid == 0)
        def _():
            place.greet(all_wide=True)
            sums_out[...] = jnp.zeros_like(sums_out)
            base = chunks * steps + chunks
            select[...] = dot_last(one_hot(nums[0:1, :], rows), one_hot(nums[1:2, :], segments)).astype(jnp.bfloat16)
            picked = jnp.dot(select[...].T, enc[...], preferred_element_type=jnp.float32).astype(jnp.bfloat16)
            leaving[...] = picked.reshape(leaving.shape)
            rows_in = exchange(leaving, arrived, base)
            pair_first, pair_second = one_hot(nums[2:3, :], segments), one_hot(nums[3:4, :], segments)
            scores = dot_last(dir_w[...], rows_in)

            def chosen(values, pairs):
                split = jnp.dot(parts_of(values, 3), pairs, preferred_element_type=jnp.float32)
                return split[:classes] + split[classes : 2 * classes] + split[2 * classes :]

            logits = chosen(scores[:classes], pair_first) + chosen(scores[classes:], pair_second) + dir_b[...]
            powers = jnp.exp(logits - jnp.max(logits, 0, keepdims=True))
            chance = powers / jnp.sum(powers, 0, keepdims=True)
            kinds = lax.broadcasted_iota(jnp.int32, logits.shape, 0)
            delta = chance - jnp.where(kinds == nums[4:5, :], 1.0, 0.0)
            sums_out[first_dir + 2 * classes : first_dir + 3 * classes, :] = jnp.broadcast_to(
                jnp.sum(delta, 1, keepdims=True), (classes, width)
            )
            split = parts_of(delta, 2)
            gathered = []
            for pairs in (pair_first, pair_second):
                both = dot_last(split, pairs)
                gathered.append(both[:classes] + both[classes:])
            per_row = parts_of(jnp.concatenate(gathered), 2)
            both = jnp.dot(per_row, rows_in, preferred_element_type=jnp.float32)
            sums_out[first_dir : first_dir + 2 * classes, :] = both[: 2 * classes] + both[2 * classes :]
            twice = jnp.concatenate([dir_w[...], dir_w[...]])
            grads = jnp.dot(per_row.T, twice, preferred_element_type=jnp.float32).astype(jnp.bfloat16)
            leaving_grads[...] = grads.reshape(leaving.shape)
            grads_in = exchange(leaving_grads, arrived_grads, base + wide - 1)

            def body(i, carry):
                at = pl.multiple_of(i * row_block, row_block)
                some = pl.ds(at, row_block)
                normed = n2[some, :].astype(jnp.float32)
                doc = at // length
                line = lax.broadcasted_iota(jnp.int32, (row_block, 1), 0) + (at - doc * length)
                grad = cot[some, :].astype(jnp.float32) + jnp.dot(
                    select[some, :], grads_in, preferred_element_type=jnp.float32
                )
                grad = jnp.where(line < lens[doc], grad, 0.0)
                two = norm_back_rows(grad, normed, q2[some, :], gain2[...])
                low = two.astype(jnp.bfloat16)
                grad_hidden[some, :] = two
                lowered[some, :] = low
                lowered_t[:, some] = low.T
                hidden_t[:, some] = hidden[some, :].T
                sums_out[0:1, :] += jnp.sum(grad * normed, 0, keepdims=True)
                sums_out[1:2, :] += jnp.sum(grad, 0, keepdims=True)
                sums_out[2:3, :] += jnp.sum(low.astype(jnp.float32), 0, keepdims=True)
                return carry

            lax.fori_loop(0, row_steps, body, 0)

        @pl.when(pid < chunks)
        def _():
            actives = jnp.concatenate([ref[...] for ref in act], axis=1)
            result = jnp.dot(lowered_t[...], actives, preferred_element_type=jnp.float32).astype(jnp.bfloat16)
            for w in range(wide):
                for n in range(narrow):
                    own[(pid,) + bits_of(w, wide_bits) + bits_of(n, narrow_bits)] = result[
                        w * d_rows : (w + 1) * d_rows, n * 128 : (n + 1) * 128
                    ]

        @pl.when(pid >= chunks)
        def _():
            slopes = jnp.concatenate([ref[...] for ref in slo], axis=1)
            downs = jnp.concatenate([ref[...] for ref in dws], axis=0)
            ups = jnp.concatenate([ref[...] for ref in uws], axis=1)
            grad_active = dot_last(lowered[...], downs)
            grad_upper = (grad_active * slopes.astype(jnp.float32)).astype(jnp.bfloat16)
            totals = jnp.sum(grad_upper.astype(jnp.float32), 0, keepdims=True)
            at = pl.ds(pl.multiple_of(chunk_of(pid - chunks) * 128, 128), 128)
            for n in range(narrow):
                sums_out[6 + n : 7 + n, at] = totals[:, n * 128 : (n + 1) * 128]
            result = jnp.dot(hidden_t[...], grad_upper, preferred_element_type=jnp.float32).astype(jnp.bfloat16)
            for n in range(narrow):
                for z in range(narrow):
                    high = bits_of(z, wide_bits - 1)
                    up_own[(pid - chunks,) + high + bits_of(n, narrow_bits)] = result[
                        n * u_rows : (n + 1) * u_rows, z * 128 : (z + 1) * 128
                    ]
            grad_hidden[...] += dot_last(grad_upper, ups)

        def advance(number, step):
            item = pieces[number]
            total = item.add(step)
            if total is None:
                item.send(step + 1)
            else:
                j = number // 2 + third * (number % 2)
                down_out[:, j * 128 : (j + 1) * 128] = total

        for number in range(chunks):
            @pl.when(pid == chunks + number)
            def _():
                up_pieces[number].send(0)

        @pl.when(pid == 2 * chunks - 1)
        def _():
            def body(i, carry):
                at = pl.multiple_of(i * row_block, row_block)
                some = pl.ds(at, row_block)
                grad, normed = grad_hidden[some, :], n1[some, :].astype(jnp.float32)
                low = norm_back_rows(grad, normed, q1[some, :], gain1[...]).astype(jnp.bfloat16)
                ga_out[some, :] = low
                sums_out[3:4, :] += jnp.sum(grad * normed, 0, keepdims=True)
                sums_out[4:5, :] += jnp.sum(grad, 0, keepdims=True)
                sums_out[5:6, :] += jnp.sum(low.astype(jnp.float32), 0, keepdims=True)
                return carry

            lax.fori_loop(0, row_steps, body, 0)

        plan = {}
        for number in range(chunks):
            for step in range(steps):
                at = number + 1 if step == 0 else chunks + number // 2 + step
                plan.setdefault(min(at, 2 * chunks - 1), []).append((step, number))
        for at in range(2 * chunks):
            @pl.when(pid == at)
            def _():
                if at < chunks:
                    pieces[at].send(0)
                if at > chunks:
                    up_pieces[at - chunks - 1].merge(0)
                    up_write(at - chunks - 1).start()
                for step, number in sorted(plan.get(at, [])):
                    advance(number, step)
                if at == 2 * chunks - 1:
                    up_pieces[chunks - 1].merge(0)
                    up_write(chunks - 1).start()
                    for number in range(chunks):
                        up_write(number).wait()
                    for item in pieces + up_pieces:
                        item.close()

    def whole(shape):
        return pl.BlockSpec(shape, lambda g: (0,) * len(shape), pipeline_mode=pl.Buffered(1))

    def slab_columns(shape, first):
        return [pl.BlockSpec(shape, lambda g, n=n: (0, n * chunks + chunk_of(g - first))) for n in range(narrow)]

    in_specs = [pl.BlockSpec(memory_space=pltpu.SMEM), whole(numbers.shape), whole((rows, width)), whole((rows, width))]
    in_specs += [whole(dir_rows.shape), whole(dir_bias.shape)]
    in_specs += [whole((rows, width)), whole((rows, 1)), whole((1, width))]
    in_specs += [whole((rows, width)), whole((rows, 1)), whole((1, width)), whole((rows, width))]
    in_specs += slab_columns((rows, 128), 0) + slab_columns((rows, 128), chunks)
    in_specs += [pl.BlockSpec((128, width), lambda g, n=n: (n * chunks + chunk_of(g - chunks), 0)) for n in range(narrow)]
    in_specs += slab_columns((width, 128), chunks)
    high = two * (wide_bits - 1)
    low = two * narrow_bits
    up_shape = (third,) + high + (2,) + low[1:] + (u_rows, 128)
    out_specs = [
        whole((rows, width)),
        pl.BlockSpec(memory_space=pl.ANY),
        whole((d_rows, chunks * 128)),
        whole((sum_rows, width)),
    ]
    out_shape = [
        jax.ShapeDtypeStruct((rows, width), jnp.bfloat16),
        jax.ShapeDtypeStruct(up_shape, jnp.bfloat16),
        jax.ShapeDtypeStruct((d_rows, chunks * 128), jnp.float32),
        jax.ShapeDtypeStruct((sum_rows, width), jnp.float32),
    ]
    scratch = [
        pltpu.VMEM((rows, width), jnp.float32),
        pltpu.VMEM((rows, width), jnp.bfloat16),
        pltpu.VMEM((width, rows), jnp.bfloat16),
        pltpu.VMEM((width, rows), jnp.bfloat16),
        pltpu.VMEM((chunks,) + two * steps + (d_rows, 128), jnp.bfloat16),
        pltpu.VMEM((chunks,) + high + low + (u_rows, 128), jnp.bfloat16),
        pltpu.VMEM((chunks,) + high + low[1:] + (u_rows, 128), jnp.bfloat16),
    ]
    scratch += [pltpu.VMEM((chunks,) + two * (steps - 1 - s) + (d_rows, 128), jnp.bfloat16) for s in range(steps)]
    scratch += [pltpu.VMEM((rows, segments), jnp.bfloat16)]
    scratch += [pltpu.VMEM((wide, segments // wide, width), jnp.bfloat16)] * 4
    sems = chunks * steps + chunks + 2 * (wide - 1)
    scratch += [pltpu.SemaphoreType.DMA((sems,)), pltpu.SemaphoreType.DMA((sems,)), pltpu.SemaphoreType.DMA((chunks,))]
    return pl.pallas_call(
        kernel,
        grid=(2 * chunks,),
        in_specs=in_specs,
        out_specs=out_specs,
        out_shape=out_shape,
        scratch_shapes=scratch,
        compiler_params=pltpu.CompilerParams(collective_id=0, has_side_effects=True, vmem_limit_bytes=58 << 20),
        name="ffn_backward",
    )(lengths, numbers, encoded, cotangent, dir_rows, dir_bias, normed_two, inverse_two, second_gain, normed_one, inverse_one, first_gain, hidden_low,
      *([active] * narrow), *([slope] * narrow), *([down_weight] * narrow), *([up_weight] * narrow))


def attention_backward(grad_attended, mixed, out_weight, qkv, totals, key_bias, tokens, qkv_weight, up_grads, sums):
    rows, width = tokens.shape
    docs, _, length = key_bias.shape
    pairs = width // 128
    names = axis_bits()
    steps = len(names)
    wide, narrow = lax.axis_size("wide"), lax.axis_size("narrow")
    wide_bits, narrow_bits = wide.bit_length() - 1, narrow.bit_length() - 1
    half = narrow // 2
    half_bits = narrow_bits - 1
    lanes = width // half
    q_rows, o_rows = 3 * width // wide // 2, width // wide // 2
    q_parts = lanes // 128
    orders = link_orders()
    ups = up_grads.shape[0]
    u_rows = up_grads.shape[-2]
    attn_steps = docs * pairs
    token_block = 256
    token_steps = rows // token_block
    first_q = 1 + attn_steps
    first_t = first_q + q_parts
    grid = first_t + token_steps
    count = ups + 1 + q_parts
    small_rows = sums.shape[0]

    def bits_of(number, count):
        return tuple((number >> bit) & 1 for bit in reversed(range(count)))

    def kernel(*refs):
        (ga, mix, ow, q_ref, k_ref, v_ref, tot_ref, bias, tok_hbm, qw_hbm, up_hbm, small) = refs[:12]
        tokens_out, up_out, out_out, qkv_out, small_out, late_out = refs[12:18]
        rest = list(refs[18:])
        gm, mix_pair, gqkv_t, up_own, out_own, qkv_own = rest[:6]
        rest = rest[6:]
        up_received, rest = rest[: steps - 1], rest[steps - 1 :]
        out_received, qkv_received, rest = rest[:steps], rest[steps : 2 * steps], rest[2 * steps :]
        small_sent, small_received, late_sent, late_received, swap_out, swap_qkv, tok, qw = rest[:8]
        send_sems, recv_sems, local_sems = rest[8:]
        pid = pl.program_id(0)
        place = Place()
        core = place.bit["narrow", 0]
        pieces = []
        for number in range(ups):
            pieces.append(Halving(place, names[:-1], orders[number % 3][1:], up_hbm.at[number], up_own.at[number],
                                  [r.at[number] for r in up_received], send_sems, recv_sems, number * steps))
        pieces.append(Halving(place, names, orders[1], out_own, out_own, out_received, send_sems, recv_sems, ups * steps))
        for number in range(q_parts):
            pieces.append(Halving(place, names, orders[number % 3], qkv_own.at[number], qkv_own.at[number],
                                  [r.at[number] for r in qkv_received], send_sems, recv_sems, (ups + 1 + number) * steps))
        base = count * steps

        def all_sum(sent, received, first):
            made = []
            for step in range(steps):
                made.append(pltpu.make_async_remote_copy(
                    src_ref=sent.at[step], dst_ref=received.at[step], send_sem=send_sems.at[first + step],
                    recv_sem=recv_sems.at[first + step], device_id=place.across(orders[0][step]),
                    device_id_type=MESH_ID))
            return made

        small_copies = all_sum(small_sent, small_received, base)
        late_copies = all_sum(late_sent, late_received, base + steps)
        swap_refs = [swap_out.at[core]] + [swap_qkv.at[number, core] for number in range(q_parts)]
        swaps = [pltpu.make_async_remote_copy(
            src_ref=ref, dst_ref=ref, send_sem=send_sems.at[base + 2 * steps + slot],
            recv_sem=recv_sems.at[base + 2 * steps + slot], device_id=place.across(("narrow", 0)),
            device_id_type=MESH_ID) for slot, ref in enumerate(swap_refs)]
        local = []
        for number in range(ups):
            keep = pieces[number].region(0, True)
            local.append(pltpu.make_async_copy(up_hbm.at[number].at[keep], up_own.at[number].at[keep], local_sems.at[number]))

        loads = [pltpu.make_async_copy(tok_hbm, tok, local_sems.at[ups]),
                 pltpu.make_async_copy(qw_hbm, qw, local_sems.at[ups + 1])]

        def advance(number, step):
            item = pieces[number]
            if step == 0 and number < ups:
                local[number].wait()
            total = item.add(step)
            if total is None:
                item.send(step + 1)
            elif number < ups:
                up_out[:, number * 128 : (number + 1) * 128] = total
            else:
                if number == ups:
                    swap_out[core] = total
                else:
                    swap_qkv[number - ups - 1, core] = total
                swaps[number - ups].start()

        def advance_small(copies, sent, received, out, step):
            copies[step].wait_recv()
            total = sent[step] + received[step]
            if step + 1 < steps:
                sent[step + 1] = total
                copies[step + 1].start()
            else:
                out[...] = total

        @pl.when(pid == 0)
        def _():
            place.greet()
            for number in range(ups):
                pieces[number].send(0)
                local[number].start()
            small_sent[0] = small[...]
            small_copies[0].start()
            for load in loads:
                load.start()
            grads_t = ga[...].T
            result = jnp.dot(grads_t, mix[...], preferred_element_type=jnp.float32).astype(jnp.bfloat16)
            for w in range(wide):
                for h in range(2):
                    for y in range(half):
                        at = (w * 2 + h) * o_rows
                        out_own[bits_of(w, wide_bits) + bits_of(y, half_bits) + (h,)] = result[
                            at : at + o_rows, y * lanes : (y + 1) * lanes
                        ]
            pieces[ups].send(0)
            grad_mixed = dot_last(ga[...], ow[...]).astype(jnp.bfloat16)
            for pair in range(pairs):
                gm[pair] = grad_mixed[:, pair * 128 : (pair + 1) * 128]
                mix_pair[pair] = mix[:, pair * 128 : (pair + 1) * 128]

        @pl.when((pid >= 1) & (pid < first_q))
        def _():
            number = pid - 1
            pair, doc = number // docs, number % docs
            some = pl.ds(pl.multiple_of(doc * length, length), length)
            lane = lax.broadcasted_iota(jnp.int32, (1, 128), 1)
            scale = jnp.bfloat16(HEAD_DIM**-0.5)
            queries, keys, values = q_ref[...] * scale, k_ref[...], v_ref[...]
            grads = gm[pair, some, :]
            product = grads.astype(jnp.float32) * mix_pair[pair, some, :].astype(jnp.float32)
            queries_t, grads_t = queries.T, grads.T
            zero = jnp.zeros_like(queries)
            query_parts = []
            for head in range(2):
                inside = (lane // HEAD_DIM) == head
                at = head * HEAD_DIM
                scores = dot_last(jnp.where(inside, queries, zero), keys) + bias[0]
                attention = jnp.exp(scores - tot_ref[:, at : at + 1])
                chance = dot_last(jnp.where(inside, grads, zero), values)
                inner = jnp.sum(jnp.where(inside, product, 0.0), -1, keepdims=True)
                grad_scores = (attention * (chance - inner)).astype(jnp.bfloat16)
                query_parts.append(jnp.dot(grad_scores, keys, preferred_element_type=jnp.float32))
                key_t = jnp.dot(queries_t[at : at + HEAD_DIM], grad_scores, preferred_element_type=jnp.float32)
                value_t = jnp.dot(grads_t[at : at + HEAD_DIM], attention.astype(jnp.bfloat16),
                                  preferred_element_type=jnp.float32)
                row = pair * 128 + at
                gqkv_t[pl.ds(pl.multiple_of(width + row, HEAD_DIM), HEAD_DIM), some] = key_t.astype(jnp.bfloat16)
                gqkv_t[pl.ds(pl.multiple_of(2 * width + row, HEAD_DIM), HEAD_DIM), some] = value_t.astype(jnp.bfloat16)
            grad_query = jnp.where(lane < HEAD_DIM, query_parts[0], query_parts[1]) * HEAD_DIM**-0.5
            gqkv_t[pl.ds(pl.multiple_of(pair * 128, 128), 128), some] = grad_query.astype(jnp.bfloat16).T

        for part in range(q_parts):
            @pl.when(pid == first_q + part)
            def _():
                if part == 0:
                    for load in loads:
                        load.wait()
                    ones = jnp.ones((8, rows), jnp.bfloat16)
                    late_sent[0] = jnp.concatenate(
                        [dot_last(ones, gqkv_t[:width, :]), dot_last(ones, gqkv_t[2 * width :, :])], axis=1
                    )
                    late_copies[0].start()
                columns = jnp.concatenate(
                    [tok[:, y * lanes + part * 128 : y * lanes + (part + 1) * 128] for y in range(half)], axis=1
                )
                result = jnp.dot(gqkv_t[...], columns, preferred_element_type=jnp.float32).astype(jnp.bfloat16)
                for w in range(wide):
                    for h in range(2):
                        for y in range(half):
                            at = (w * 2 + h) * q_rows
                            qkv_own[(part,) + bits_of(w, wide_bits) + bits_of(y, half_bits) + (h,)] = result[
                                at : at + q_rows, y * 128 : (y + 1) * 128
                            ]
                pieces[ups + 1 + part].send(0)

        @pl.when(pid >= first_t)
        def _():
            at = pl.multiple_of((pid - first_t) * token_block, token_block)
            some = pl.ds(at, token_block)
            grad_t = jnp.dot(qw[...], gqkv_t[:, some], preferred_element_type=jnp.float32)
            tokens_out[some, :] = (grad_t.T + ga[some, :].astype(jnp.float32)).astype(jnp.bfloat16)

        plan, small_plan, late_plan = {}, {}, {}
        for step, at in enumerate((4, 7, 8, 11)):
            for number in range(ups):
                plan.setdefault(at, []).append((number, step))
        for step, at in enumerate((1, 7, 9, 10, 12)):
            plan.setdefault(at, []).append((ups, step))
        for part in range(q_parts):
            for step in range(steps):
                plan.setdefault(first_q + part + 1 if step == 0 else grid - 1, []).append((ups + 1 + part, step))
        for step, at in enumerate((2, 3, 5, 7, 9)):
            small_plan[at] = step
        for step in range(steps):
            late_plan[first_q + 1 + step] = step
        for at in range(grid):
            @pl.when(pid == at)
            def _():
                if at in small_plan:
                    advance_small(small_copies, small_sent, small_received, small_out, small_plan[at])
                for number, step in sorted(plan.get(at, []), key=lambda entry: (entry[1], entry[0])):
                    advance(number, step)
                if at in late_plan:
                    advance_small(late_copies, late_sent, late_received, late_out, late_plan[at])
                if at == grid - 1:
                    for copy in swaps:
                        copy.wait()
                    out_out[...] = swap_out[...]
                    qkv_out[...] = swap_qkv[...]
                    for item in pieces:
                        item.close()
                    for copy in small_copies + late_copies:
                        copy.wait_send()

    def whole(shape):
        return pl.BlockSpec(shape, lambda g: (0,) * len(shape), pipeline_mode=pl.Buffered(1))

    def number_of(g):
        return jnp.clip(g - 1, 0, attn_steps - 1)

    def tile(which):
        return pl.BlockSpec((length, 128), lambda g: (number_of(g) % docs, which * pairs + number_of(g) // docs))

    two = (2,)
    any_space = pl.BlockSpec(memory_space=pl.ANY)
    in_specs = [whole((rows, width)), whole((rows, width)), whole((width, width)), tile(0), tile(1), tile(2), tile(0)]
    in_specs += [pl.BlockSpec((1, 1, length), lambda g: (number_of(g) % docs, 0, 0)), any_space]
    in_specs += [any_space, any_space, whole((small_rows, width))]
    out_shape = [
        jax.ShapeDtypeStruct((rows, width), jnp.bfloat16),
        jax.ShapeDtypeStruct((u_rows, ups * 128), jnp.float32),
        jax.ShapeDtypeStruct((2, o_rows, lanes), jnp.float32),
        jax.ShapeDtypeStruct((q_parts, 2, q_rows, 128), jnp.float32),
        jax.ShapeDtypeStruct((small_rows, width), jnp.float32),
        jax.ShapeDtypeStruct((8, 2 * width), jnp.float32),
    ]
    wide_dims, half_dims = two * wide_bits, two * half_bits
    scratch = [
        pltpu.VMEM((pairs, rows, 128), jnp.bfloat16),
        pltpu.VMEM((pairs, rows, 128), jnp.bfloat16),
        pltpu.VMEM((3 * width, rows), jnp.bfloat16),
        pltpu.VMEM(up_grads.shape, jnp.bfloat16),
        pltpu.VMEM(wide_dims + half_dims + two + (o_rows, lanes), jnp.bfloat16),
        pltpu.VMEM((q_parts,) + wide_dims + half_dims + two + (q_rows, 128), jnp.bfloat16),
    ]
    scratch += [pltpu.VMEM((ups,) + two * (steps - 2 - s) + (u_rows, 128), jnp.bfloat16) for s in range(steps - 1)]
    scratch += [pltpu.VMEM(two * (steps - 1 - s) + (o_rows, lanes), jnp.bfloat16) for s in range(steps)]
    scratch += [pltpu.VMEM((q_parts,) + two * (steps - 1 - s) + (q_rows, 128), jnp.bfloat16) for s in range(steps)]
    scratch += [pltpu.VMEM((steps, small_rows, width), jnp.float32)] * 2
    scratch += [pltpu.VMEM((steps, 8, 2 * width), jnp.float32)] * 2
    scratch += [pltpu.VMEM(out_shape[2].shape, jnp.float32), pltpu.VMEM(out_shape[3].shape, jnp.float32)]
    scratch += [pltpu.VMEM(tokens.shape, jnp.bfloat16), pltpu.VMEM(qkv_weight.shape, jnp.bfloat16)]
    sems = count * steps + 2 * steps + 1 + q_parts
    scratch += [pltpu.SemaphoreType.DMA((sems,)), pltpu.SemaphoreType.DMA((sems,)), pltpu.SemaphoreType.DMA((ups + 2,))]
    return pl.pallas_call(
        kernel,
        grid=(grid,),
        in_specs=in_specs,
        out_specs=[whole(item.shape) for item in out_shape],
        out_shape=out_shape,
        scratch_shapes=scratch,
        compiler_params=pltpu.CompilerParams(collective_id=1, has_side_effects=True, vmem_limit_bytes=60 << 20),
        name="attention_backward",
    )(grad_attended, mixed, out_weight, qkv, qkv, qkv, totals, key_bias, tokens, qkv_weight, up_grads, sums)


def on_device_fast(
    tokens,
    doc_lengths,
    qkv_weight,
    query_bias,
    value_bias,
    out_weight,
    out_bias,
    first_gain,
    first_shift,
    up_weight,
    up_bias,
    down_weight,
    down_bias,
    second_gain,
    second_shift,
    dir_weight,
    dir_bias,
    segment_rows,
    segment_slots,
    pair_rows,
    pair_labels,
    out_cotangent,
):
    doc_count, length, model_width = tokens.shape
    low = jnp.bfloat16
    token_rows = tokens.reshape(doc_count * length, model_width)
    allowed = lax.broadcasted_iota(jnp.int32, (doc_count, length), 1) < doc_lengths[:, None]
    key_bias = jnp.where(allowed, 0.0, MASKED).astype(jnp.float32).reshape(doc_count, 1, length)
    allowed_rows = allowed.reshape(-1, 1).astype(jnp.float32)
    bias_row = jnp.concatenate([query_bias, jnp.zeros_like(query_bias), value_bias]).astype(jnp.float32)
    qkv = (jnp.dot(token_rows, qkv_weight, preferred_element_type=jnp.float32) + bias_row).astype(low)
    mixed, totals = attention_forward(qkv, key_bias, doc_count, length)
    attended = jnp.dot(mixed, out_weight, preferred_element_type=jnp.float32) + out_bias.astype(jnp.float32)
    resid_one = token_rows.astype(jnp.float32) + attended
    hidden_one, normed_one, inverse_one = norm_forward(
        resid_one, first_gain.astype(jnp.float32), first_shift.astype(jnp.float32)
    )
    hidden_low = hidden_one.astype(low)
    upper_pre = jnp.dot(hidden_low, up_weight, preferred_element_type=jnp.float32) + up_bias.astype(jnp.float32)
    cumulative = normal_cdf(upper_pre)
    active = (upper_pre * cumulative).astype(low)
    density = jnp.exp(-0.5 * upper_pre * upper_pre) * 0.3989422804014327
    slope = (cumulative + upper_pre * density).astype(low)
    lowered = jnp.dot(active, down_weight, preferred_element_type=jnp.float32) + down_bias.astype(jnp.float32)
    resid_two = hidden_one + lowered
    second_float = second_gain.astype(jnp.float32)
    normed_out, normed_two, inverse_two = norm_forward(resid_two, second_float, second_shift.astype(jnp.float32))
    encoded_rows = (normed_out * allowed_rows).astype(low)
    classes_count = dir_weight.shape[1]
    doc_starts = lax.broadcasted_iota(jnp.int32, (doc_count, 1), 0) * length
    numbers = jnp.concatenate(
        [(segment_rows + doc_starts).reshape(1, -1), segment_slots, pair_rows[:, :, 0], pair_rows[:, :, 1], pair_labels]
    )
    numbers = jnp.pad(numbers, ((0, -numbers.shape[0] % 8), (0, 0)))
    dir_rows = dir_weight.reshape(2, model_width, classes_count).transpose(0, 2, 1).reshape(-1, model_width)
    grad_attended, up_blocks, out_down, sums = ffn_backward(
        doc_lengths, numbers, encoded_rows, out_cotangent.reshape(-1, model_width), dir_rows,
        dir_bias.astype(jnp.float32)[:, None], normed_two.astype(low), inverse_two, second_float[None], active, slope,
        hidden_low, down_weight, up_weight, normed_one.astype(low), inverse_one, first_gain.astype(jnp.float32)[None],
    )
    grad_tokens, out_up, out_out, out_qkv, sums, late = attention_backward(
        grad_attended, mixed, out_weight, qkv, totals, key_bias, token_rows, qkv_weight, up_blocks, sums
    )
    core = lax.axis_index("narrow") % 2
    width = model_width // lax.axis_size("narrow")
    out_qkv = out_qkv.transpose(1, 2, 0, 3).reshape(-1, 2 * width)
    out_out = out_out.reshape(-1, 2 * width)

    def own_lanes(rows):
        return lax.dynamic_slice_in_dim(rows, core * width, width, 1).T

    first_dir = 6 + lax.axis_size("narrow")
    last_dir = first_dir + 2 * classes_count
    dir_sum = sums[first_dir:last_dir].reshape(2, classes_count, model_width).transpose(0, 2, 1)
    return (
        encoded_rows.reshape(tokens.shape),
        grad_tokens.reshape(tokens.shape),
        own_lanes(out_qkv),
        late[0, :model_width],
        late[0, model_width:],
        own_lanes(out_out),
        sums[5],
        sums[3],
        sums[4],
        out_up,
        sums[6:first_dir].reshape(-1),
        out_down.T,
        sums[2],
        sums[0],
        sums[1],
        dir_sum.reshape(2 * model_width, classes_count),
        sums[last_dir : last_dir + classes_count, 0],
    )


def on_device(
    tokens,
    doc_lengths,
    qkv_weight,
    query_bias,
    value_bias,
    out_weight,
    out_bias,
    first_gain,
    first_shift,
    up_weight,
    up_bias,
    down_weight,
    down_bias,
    second_gain,
    second_shift,
    dir_weight,
    dir_bias,
    segment_rows,
    segment_slots,
    pair_rows,
    pair_labels,
    out_cotangent,
):
    doc_count, length, model_width = tokens.shape
    score_scale = HEAD_DIM ** (-0.5)
    token_rows = tokens.reshape(doc_count * length, model_width)
    allowed = lax.broadcasted_iota(jnp.int32, (doc_count, length), 1) < doc_lengths[:, None]
    allowed_rows = allowed.reshape(-1, 1).astype(jnp.float32)
    bias_row = jnp.concatenate([query_bias, jnp.zeros_like(query_bias), value_bias]).astype(
        jnp.float32
    )
    qkv = (jnp.dot(token_rows, qkv_weight, preferred_element_type=jnp.float32) + bias_row).astype(
        jnp.bfloat16
    )

    def split_heads(doc_block, which):
        return doc_block[:, which * model_width : (which + 1) * model_width].reshape(
            length, HEADS, HEAD_DIM
        )

    def scores_of(queries, key_rows, doc_mask):
        scores = (
            jnp.einsum("qhd,khd->hqk", queries, key_rows, preferred_element_type=jnp.float32)
            * score_scale
        )
        return jnp.where(doc_mask[None, None, :], scores, MASKED)

    mixed_parts = []
    log_totals = []
    for doc_index in range(doc_count):
        doc_block = qkv[doc_index * length : (doc_index + 1) * length]
        queries = split_heads(doc_block, 0)
        key_rows = split_heads(doc_block, 1)
        value_rows = split_heads(doc_block, 2)
        scores = scores_of(queries, key_rows, allowed[doc_index])
        highest = jnp.max(scores, -1, keepdims=True)
        powers = jnp.exp(scores - highest)
        summed = jnp.sum(powers, -1, keepdims=True)
        attention = (powers / summed).astype(jnp.bfloat16)
        log_totals.append(highest + jnp.log(summed))
        mixed_parts.append(
            jnp.einsum(
                "hqk,khd->qhd", attention, value_rows, preferred_element_type=jnp.float32
            ).reshape(length, model_width)
        )
    mixed = jnp.concatenate(mixed_parts).astype(jnp.bfloat16)
    attended = jnp.dot(mixed, out_weight, preferred_element_type=jnp.float32) + out_bias.astype(
        jnp.float32
    )
    resid_one = token_rows.astype(jnp.float32) + attended
    hidden_one, normed_one, inverse_one = norm_forward(
        resid_one, first_gain.astype(jnp.float32), first_shift.astype(jnp.float32)
    )
    hidden_low = hidden_one.astype(jnp.bfloat16)
    upper_pre = jnp.dot(hidden_low, up_weight, preferred_element_type=jnp.float32) + up_bias.astype(
        jnp.float32
    )
    cumulative = normal_cdf(upper_pre)
    active = (upper_pre * cumulative).astype(jnp.bfloat16)
    lowered = jnp.dot(active, down_weight, preferred_element_type=jnp.float32) + down_bias.astype(
        jnp.float32
    )
    resid_two = hidden_one + lowered
    second_float = second_gain.astype(jnp.float32)
    normed_out, normed_two, inverse_two = norm_forward(
        resid_two, second_float, second_shift.astype(jnp.float32)
    )
    encoded_rows = (normed_out * allowed_rows).astype(jnp.bfloat16)
    doc_starts = lax.broadcasted_iota(jnp.int32, (doc_count, 1), 0) * length
    picked_rows = (segment_rows + doc_starts).reshape(-1)
    picked = encoded_rows[picked_rows]
    slots = segment_slots.reshape(-1)
    outgoing = jnp.zeros_like(picked).at[slots].set(picked)
    arrived = lax.all_to_all(outgoing, "wide", split_axis=0, concat_axis=0, tiled=True)
    pairs = pair_rows.reshape(-1, 2)
    labels = pair_labels.reshape(-1)
    first_rows = arrived[pairs[:, 0]]
    second_rows = arrived[pairs[:, 1]]
    logits = (
        jnp.dot(first_rows, dir_weight[:model_width], preferred_element_type=jnp.float32)
        + jnp.dot(second_rows, dir_weight[model_width:], preferred_element_type=jnp.float32)
        + dir_bias.astype(jnp.float32)
    )
    powers_head = jnp.exp(logits - jnp.max(logits, -1, keepdims=True))
    chance = powers_head / jnp.sum(powers_head, -1, keepdims=True)
    classes = lax.broadcasted_iota(jnp.int32, logits.shape, 1)
    delta = chance - (labels[:, None] == classes).astype(jnp.float32)
    first_float = first_rows.astype(jnp.float32)
    second_rows_float = second_rows.astype(jnp.float32)
    grad_dir_weight = jnp.concatenate(
        [
            jnp.dot(first_float.T, delta, precision=EXACT, preferred_element_type=jnp.float32),
            jnp.dot(
                second_rows_float.T, delta, precision=EXACT, preferred_element_type=jnp.float32
            ),
        ]
    )
    grad_dir_bias = jnp.sum(delta, 0)
    dir_float = dir_weight.astype(jnp.float32)
    grad_first = jnp.dot(
        delta, dir_float[:model_width].T, precision=EXACT, preferred_element_type=jnp.float32
    )
    grad_second = jnp.dot(
        delta, dir_float[model_width:].T, precision=EXACT, preferred_element_type=jnp.float32
    )
    grad_arrived = jnp.zeros((arrived.shape[0], model_width), jnp.float32)
    grad_arrived = grad_arrived.at[pairs[:, 0]].add(grad_first).at[pairs[:, 1]].add(grad_second)
    returned = lax.all_to_all(
        grad_arrived.astype(jnp.bfloat16), "wide", split_axis=0, concat_axis=0, tiled=True
    )
    grad_picked = returned[slots].astype(jnp.float32)
    grad_encoded = (
        out_cotangent.reshape(-1, model_width).astype(jnp.float32).at[picked_rows].add(grad_picked)
    )
    grad_encoded = grad_encoded * allowed_rows
    grad_two, grad_second_gain, grad_second_shift = norm_backward(
        grad_encoded, normed_two, inverse_two, second_float
    )
    grad_lowered = grad_two.astype(jnp.bfloat16)
    grad_down_weight = jnp.einsum(
        "rf,rd->fd", active, grad_lowered, preferred_element_type=jnp.float32
    )
    grad_down_bias = jnp.sum(grad_lowered.astype(jnp.float32), 0)
    grad_active = jnp.einsum(
        "rd,fd->rf", grad_lowered, down_weight, preferred_element_type=jnp.float32
    )
    density = jnp.exp(-0.5 * upper_pre * upper_pre) * 0.3989422804014327
    grad_upper = (grad_active * (cumulative + upper_pre * density)).astype(jnp.bfloat16)
    grad_up_weight = jnp.einsum(
        "rd,rf->df", hidden_low, grad_upper, preferred_element_type=jnp.float32
    )
    grad_up_bias = jnp.sum(grad_upper.astype(jnp.float32), 0)
    grad_hidden = grad_two + jnp.einsum(
        "rf,df->rd", grad_upper, up_weight, preferred_element_type=jnp.float32
    )
    grad_one, grad_first_gain, grad_first_shift = norm_backward(
        grad_hidden, normed_one, inverse_one, first_gain.astype(jnp.float32)
    )
    grad_attended = grad_one.astype(jnp.bfloat16)
    grad_out_weight = jnp.einsum(
        "rd,re->de", mixed, grad_attended, preferred_element_type=jnp.float32
    )
    grad_out_bias = jnp.sum(grad_attended.astype(jnp.float32), 0)
    grad_mixed = jnp.einsum(
        "re,de->rd", grad_attended, out_weight, preferred_element_type=jnp.float32
    ).astype(jnp.bfloat16)
    grad_parts = []
    for doc_index in range(doc_count):
        doc_block = qkv[doc_index * length : (doc_index + 1) * length]
        queries = split_heads(doc_block, 0)
        key_rows = split_heads(doc_block, 1)
        value_rows = split_heads(doc_block, 2)
        scores = scores_of(queries, key_rows, allowed[doc_index])
        attention = jnp.exp(scores - log_totals[doc_index])
        grad_doc = grad_mixed[doc_index * length : (doc_index + 1) * length].reshape(
            length, HEADS, HEAD_DIM
        )
        grad_chance = jnp.einsum(
            "qhd,khd->hqk", grad_doc, value_rows, preferred_element_type=jnp.float32
        )
        inner = jnp.sum(grad_chance * attention, -1, keepdims=True)
        grad_scores = (attention * (grad_chance - inner)).astype(jnp.bfloat16)
        grad_query = (
            jnp.einsum("hqk,khd->qhd", grad_scores, key_rows, preferred_element_type=jnp.float32)
            * score_scale
        )
        grad_key = (
            jnp.einsum("hqk,qhd->khd", grad_scores, queries, preferred_element_type=jnp.float32)
            * score_scale
        )
        grad_value = jnp.einsum(
            "hqk,qhd->khd",
            attention.astype(jnp.bfloat16),
            grad_doc,
            preferred_element_type=jnp.float32,
        )
        grad_parts.append(
            jnp.concatenate(
                [
                    grad_query.reshape(length, model_width),
                    grad_key.reshape(length, model_width),
                    grad_value.reshape(length, model_width),
                ],
                axis=1,
            )
        )
    grad_qkv = jnp.concatenate(grad_parts).astype(jnp.bfloat16)
    grad_qkv_float = grad_qkv.astype(jnp.float32)
    grad_query_bias = jnp.sum(grad_qkv_float[:, :model_width], 0)
    grad_value_bias = jnp.sum(grad_qkv_float[:, 2 * model_width :], 0)
    grad_qkv_weight = jnp.einsum(
        "rd,re->de", token_rows, grad_qkv, preferred_element_type=jnp.float32
    )
    grad_tokens = (
        jnp.einsum("re,de->rd", grad_qkv, qkv_weight, preferred_element_type=jnp.float32) + grad_one
    ).astype(jnp.bfloat16)
    matrices = (grad_qkv_weight, grad_out_weight, grad_up_weight, grad_down_weight)
    partial_sums = (
        lax.psum_scatter(
            matrices[0].astype(jnp.bfloat16), "wide", scatter_dimension=1, tiled=True
        ).astype(jnp.float32),
        lax.psum_scatter(
            matrices[1].astype(jnp.bfloat16), "wide", scatter_dimension=1, tiled=True
        ).astype(jnp.float32),
        lax.psum_scatter(
            matrices[2].astype(jnp.bfloat16), "wide", scatter_dimension=1, tiled=True
        ).astype(jnp.float32),
        lax.psum_scatter(
            matrices[3].astype(jnp.bfloat16), "wide", scatter_dimension=1, tiled=True
        ).astype(jnp.float32),
    )
    summed_mats = (
        lax.psum_scatter(
            partial_sums[0].astype(jnp.bfloat16), "narrow", scatter_dimension=0, tiled=True
        ).astype(jnp.float32),
        lax.psum_scatter(
            partial_sums[1].astype(jnp.bfloat16), "narrow", scatter_dimension=0, tiled=True
        ).astype(jnp.float32),
        lax.psum_scatter(
            partial_sums[2].astype(jnp.bfloat16), "narrow", scatter_dimension=0, tiled=True
        ).astype(jnp.float32),
        lax.psum_scatter(
            partial_sums[3].astype(jnp.bfloat16), "narrow", scatter_dimension=0, tiled=True
        ).astype(jnp.float32),
    )
    smalls = lax.psum(
        (
            grad_query_bias,
            grad_value_bias,
            grad_out_bias,
            grad_first_gain,
            grad_first_shift,
            grad_up_bias,
            grad_down_bias,
            grad_second_gain,
            grad_second_shift,
            grad_dir_weight,
            grad_dir_bias,
        ),
        ("wide", "narrow"),
    )
    return (
        encoded_rows.reshape(tokens.shape),
        grad_tokens.reshape(tokens.shape),
        summed_mats[0],
        smalls[0],
        smalls[1],
        summed_mats[1],
        smalls[2],
        smalls[3],
        smalls[4],
        summed_mats[2],
        smalls[5],
        summed_mats[3],
        smalls[6],
        smalls[7],
        smalls[8],
        smalls[9],
        smalls[10],
    )


def fits_blocks(mesh):
    wide, narrow = mesh.shape["wide"], mesh.shape["narrow"]
    width, ff = HEADS * HEAD_DIM, 4 * HEADS * HEAD_DIM
    if wide != 2 * narrow or narrow < 4 or narrow & (narrow - 1):
        return False
    lanes = (ff // narrow, ff // wide, 2 * width // narrow)
    rows = (width // wide, width // narrow, width // wide // 2, 3 * width // wide // 2)
    return all(size % 128 == 0 for size in lanes) and all(size % 16 == 0 for size in rows)


def solution(mesh):
    placed = (
        P(("wide", "narrow"), None, None),
        P(("wide", "narrow")),
        P(),
        P(),
        P(),
        P(),
        P(),
        P(),
        P(),
        P(),
        P(),
        P(),
        P(),
        P(),
        P(),
        P(),
        P(),
        P(("wide", "narrow"), None),
        P(("wide", "narrow"), None),
        P(("wide", "narrow"), None, None),
        P(("wide", "narrow"), None),
        P(("wide", "narrow"), None, None),
    )
    return jax.shard_map(
        on_device_fast if fits_blocks(mesh) else on_device,
        mesh=mesh,
        in_specs=placed,
        out_specs=(
            P(("wide", "narrow"), None, None),
            P(("wide", "narrow"), None, None),
            P("narrow", "wide"),
            P(),
            P(),
            P("narrow", "wide"),
            P(),
            P(),
            P(),
            P("narrow", "wide"),
            P(),
            P("narrow", "wide"),
            P(),
            P(),
            P(),
            P(),
            P(),
        ),
        check_vma=False,
    )
```

profile of v0, /device:TPU:0, one launch (start us, length us, event | category | flops | bytes accessed | tf_op | source)
XLA Modules:
  0.0 234.2 jit_solution(16439932634692206979)
XLA Ops:
  0.7 0.7 maximum_convert_fusion
  1.4 8.4 %add_convert_fusion.q_ref.k_ref.v_ref.refs_3_.refs_4_.refs_5_ = bf16[1024,2304]{1,0:T(8,128)(2,1)} fusion(bf16[1024,768]{1,0:T(8,128)(2,1)} %bitcast.52, bf16[768,2304]{1,0:T(8,128)(2,1)} %refs_9_.1, f32[2304]{0:T(1024)S(1)} %maximum_convert_fusion), kind=kOutput, calls=%fused_computation.8 | convolution fusion | flops 3628597248 | bytes 9839616 | tf_op jit(solution)/shard_map/dot_general | solution.py:781
  9.9 15.2 %attention_forward.1 = (bf16[1024,768]{1,0:T(8,128)(2,1)S(1)}, f32[1024,768]{1,0:T(8,128)S(1)}) custom-call(bf16[1024,2304]{1,0:T(8,128)(2,1)} %add_convert_fusion.q_ref.k_ref.v_ref.refs_3_.refs_4_.refs_5_, bf16[1024,2304]{1,0:T(8,128)(2,1)} %add_convert_fusion.q_ref.k_ref.v_ref.refs_3_.refs_4_.refs_5_, ...), custom_call_target="tpu_custom_call" | custom-call | tf_op jit(solution)/shard_map/attention_forward/pallas_call | solution.py:160
  25.2 1.6 fusion.7
  27.9 1.8 multiply_convert_fusion.3
  29.8 12.9 %fusion.4 = (bf16[1024,3072]{1,0:T(8,128)(2,1)}, bf16[1024,3072]{1,0:T(8,128)(2,1)S(1)}) fusion(f32[3072]{0:T(1024)S(1)} %convert_element_type.72, bf16[1024,768]{1,0:T(8,128)(2,1)S(1)} %get-tuple-element.69.refs_12_, bf16[768,3072]{1,0:T(8,128)(2,1)S(1)} %bitcast.47), kind=kOutput, calls=%fused_computation.5 | convolution fusion | flops 4869586944 | bytes 18886656 | tf_op jit(solution)/shard_map/dot_general | solution.py:789
  42.7 5.5 %fusion.8 = (f32[1024]{0:T(1024)S(1)}, f32[1024,768]{1,0:T(8,128)S(1)}) fusion(f32[768]{0:T(1024)S(1)} %convert_element_type.74, bf16[1024,3072]{1,0:T(8,128)(2,1)S(1)} %get-tuple-element.67.refs_13_.refs_14_.refs_15_.refs_16_, bf16[3072,768]{1,0:T(8,128)(2,1)S(1)} %bitcast.49, f32[768]{0:T(1024)S(1)} %convert_element_type.70, ...), kind=kOutput, calls=%fused_computation.44 | convolution fusion | flops 4837342208 | bytes 17323008 | tf_op jit(solution)/shard_map/dot_general | solution.py:794
  49.0 2.1 multiply_convert_fusion.2
  51.1 1.0 copy.42.refs_7_
  52.1 1.1 copy.43.refs_10_
  53.3 0.6 pad.4.refs_1_
  53.9 0.7 copy.41.refs_5_
  55.8 78.2 %ffn_backward.1 = (bf16[1024,768]{1,0:T(8,128)(2,1)}, bf16[3,2,2,2,2,192,128]{6,5,4,3,2,1,0:T(8,128)(2,1)}, f32[96,768]{1,0:T(8,128)}, f32[40,768]{1,0:T(8,128)}) custom-call(s32[2]{0:T(128)} %refs_0_.1, s32[8,256]{1,0:T(8,128)} %pad.4.refs_1_, bf16[1024,768]{1,0:T(8,128)(2,1)} %get-tuple-element.71.refs_2_, bf16[1024,768]{1,0:T(8,128)(2,1)} %bitcast.56, ...), custom_call_target="tpu_custom_call" | custom-call | tf_op jit(solution)/shard_map/ffn_backward/pallas_call | solution.py:466
  133.9 90.9 %attention_backward.1 = (bf16[1024,768]{1,0:T(8,128)(2,1)}, f32[192,384]{1,0:T(8,128)}, f32[2,48,384]{2,1,0:T(8,128)}, f32[3,2,144,128]{3,2,1,0:T(8,128)}, f32[40,768]{1,0:T(8,128)}, /*index=5*/f32[8,1536]{1,0:T(8,128)}) custom-call(bf16[1024,768]{1,0:T(8,128)(2,1)} %get-tuple-element.30.refs_0_, bf16[1024,768]{1,0:T(8,128)(2,1)} %copy-done.1, ...), custom_call_target="tpu_custom_call" | custom-call | tf_op jit(solution)/shard_map/attention_backward/pallas_call | solution.py:738
  224.8 1.7 slice_reduce_fusion.1
  226.5 1.3 copy.44
  228.1 0.9 copy.46
  229.0 0.7 copy.47
  229.8 0.6 slice.50
  230.4 0.6 reshape.207
  231.0 0.6 slice_reduce_fusion
  231.7 1.1 copy.55
  232.8 0.7 copy.56
  233.5 0.7 copy.57
  (88 shorter events, 3.6 us)
Async XLA Ops:
  1.4 8.4 %copy-start.15 = (s32[2]{0:T(128)S(1)}, s32[2]{0:T(128)}, u32[]{:S(2)}) copy-start(s32[2]{0:T(128)} %refs_0_.1) | copy-start | bytes 28
  9.9 15.2 %copy-start.2 = (f32[2,1,512]{2,1,0:T(1,128)}, f32[2,1,512]{2,1,0:T(1,128)S(1)}, u32[]{:S(2)}) copy-start(f32[2,1,512]{2,1,0:T(1,128)S(1)} %compare_select_fusion.bias_ref.refs_7_) | copy-start | bytes 12292
  9.9 15.3 %copy-start.16 = (bf16[768]{0:T(1024)(128)(2,1)S(1)}, bf16[768]{0:T(1024)(128)(2,1)}, u32[]{:S(2)}) copy-start(bf16[768]{0:T(1024)(128)(2,1)} %param.28) | copy-start | bytes 4612
  9.9 15.3 %copy-start.5 = (bf16[2,512,768]{2,1,0:T(8,128)(2,1)S(1)}, bf16[2,512,768]{2,1,0:T(8,128)(2,1)}, u32[]{:S(2)}) copy-start(bf16[2,512,768]{2,1,0:T(8,128)(2,1)} %param.22) | copy-start | bytes 4718596
  9.9 15.3 %copy-start.7 = (bf16[768,768]{1,0:T(8,128)(2,1)S(1)}, bf16[768,768]{1,0:T(8,128)(2,1)}, u32[]{:S(2)}) copy-start(bf16[768,768]{1,0:T(8,128)(2,1)} %refs_2_.1) | copy-start | bytes 3538948
  9.9 19.8 %slice-start = ((s8[4718592]{0:T(1024)(128)(4,1)}), s8[4194304]{0:T(1024)(128)(4,1)S(1)}, s32[]{:S(2)}) async-start(s8[4718592]{0:T(1024)(128)(4,1)} %bitcast.46), calls=%async_computation | async-start | bytes 8388608
  25.1 2.1 copy-start.1
  25.2 4.6 %slice-start.1 = ((s8[4718592]{0:T(1024)(128)(4,1)}), s8[524288]{0:T(1024)(128)(4,1)S(1)}, s32[]{:S(2)}) async-start(s8[4718592]{0:T(1024)(128)(4,1)} %bitcast.46), calls=%async_computation.1 | async-start | bytes 1048576
  27.9 1.8 copy-start.14
  27.9 14.8 %slice-start.2 = ((s8[4718592]{0:T(1024)(128)(4,1)}), s8[4194304]{0:T(1024)(128)(4,1)S(1)}, s32[]{:S(2)}) async-start(s8[4718592]{0:T(1024)(128)(4,1)} %bitcast.48), calls=%async_computation.2 | async-start | bytes 8388608
  29.7 13.0 %copy-start.4 = (bf16[1024,768]{1,0:T(8,128)(2,1)}, bf16[1024,768]{1,0:T(8,128)(2,1)S(1)}, u32[]{:S(2)}) copy-start(bf16[1024,768]{1,0:T(8,128)(2,1)S(1)} %get-tuple-element.69.refs_12_) | copy-start | bytes 4718596
  29.7 13.0 %copy-start.18 = (bf16[768]{0:T(1024)(128)(2,1)S(1)}, bf16[768]{0:T(1024)(128)(2,1)}, u32[]{:S(2)}) copy-start(bf16[768]{0:T(1024)(128)(2,1)} %param.34) | copy-start | bytes 4612
  29.7 13.0 %slice-start.3 = ((s8[4718592]{0:T(1024)(128)(4,1)}), s8[524288]{0:T(1024)(128)(4,1)S(1)}, s32[]{:S(2)}) async-start(s8[4718592]{0:T(1024)(128)(4,1)} %bitcast.48), calls=%async_computation.3 | async-start | bytes 1048576
  42.7 5.5 %copy-start.3 = (bf16[1024,3072]{1,0:T(8,128)(2,1)}, bf16[1024,3072]{1,0:T(8,128)(2,1)S(1)}, u32[]{:S(2)}) copy-start(bf16[1024,3072]{1,0:T(8,128)(2,1)S(1)} %get-tuple-element.67.refs_13_.refs_14_.refs_15_.refs_16_) | copy-start | bytes 18874372
  48.9 4.3 %copy-start.20 = (s32[1,256,2]{1,2,0:T(2,128)S(1)}, s32[1,256,2]{1,2,0:T(2,128)}, u32[]{:S(2)}) copy-start(s32[1,256,2]{1,2,0:T(2,128)} %param.41) | copy-start | bytes 6148
  48.9 4.3 %copy-start.21 = (s32[2,128]{1,0:T(2,128)S(1)}, s32[2,128]{1,0:T(2,128)}, u32[]{:S(2)}) copy-start(s32[2,128]{1,0:T(2,128)} %param.39) | copy-start | bytes 3076
  48.9 4.4 %copy-start.22 = (s32[1,256]{1,0:T(1,128)S(1)}, s32[1,256]{1,0:T(1,128)}, u32[]{:S(2)}) copy-start(s32[1,256]{1,0:T(1,128)} %param.40) | copy-start | bytes 3076
  48.9 4.4 %copy-start.23 = (s32[1,256]{1,0:T(1,128)S(1)}, s32[1,256]{1,0:T(1,128)}, u32[]{:S(2)}) copy-start(s32[1,256]{1,0:T(1,128)} %param.42) | copy-start | bytes 3076
  49.0 5.0 %copy-start.24 = (bf16[8]{0:T(256)(128)(2,1)S(1)}, bf16[8]{0:T(256)(128)(2,1)}, u32[]{:S(2)}) copy-start(bf16[8]{0:T(256)(128)(2,1)} %param.38) | copy-start | bytes 52
  224.8 4.1 %copy-start.10 = (f32[2,48,384]{2,1,0:T(8,128)S(1)}, f32[2,48,384]{2,1,0:T(8,128)}, u32[]{:S(2)}) copy-start(f32[2,48,384]{2,1,0:T(8,128)} %get-tuple-element.37) | copy-start | bytes 442372
  224.8 5.0 %copy-start.11 = (f32[40,768]{1,0:T(8,128)S(1)}, f32[40,768]{1,0:T(8,128)}, u32[]{:S(2)}) copy-start(f32[40,768]{1,0:T(8,128)} %get-tuple-element.38) | copy-start | bytes 368644
  224.8 6.8 %copy-start.6 = (bf16[1024,768]{1,0:T(8,128)(2,1)S(1)}, bf16[1024,768]{1,0:T(8,128)(2,1)}, u32[]{:S(2)}) copy-start(bf16[1024,768]{1,0:T(8,128)(2,1)} %get-tuple-element.34) | copy-start | bytes 4718596
  227.8 5.0 %copy-start.9 = (f32[192,384]{1,0:T(8,128)S(1)}, f32[192,384]{1,0:T(8,128)}, u32[]{:S(2)}) copy-start(f32[192,384]{1,0:T(8,128)} %get-tuple-element.106) | copy-start | bytes 884740
  227.9 5.7 %copy-start.8 = (f32[96,768]{1,0:T(8,128)S(1)}, f32[96,768]{1,0:T(8,128)}, u32[]{:S(2)}) copy-start(f32[96,768]{1,0:T(8,128)} %get-tuple-element.40) | copy-start | bytes 884740
  (5 other events, 4.4 us)
where the time goes:
time: 235 us; the launch traced here: 234 us
  Pallas kernels  184 us (78%)
  matrix products  28.4 us (12%)
  local copies, waits for them, and re-layouts  14.7 us (6%)
  other arithmetic  5.89 us (3%)
    pallas_call x1, Pallas kernels, attention_backward(): pl.pallas_call(kernel, grid=(grid,), in_specs=in_specs, out_specs=[whole(...  90.9 us
    pallas_call x1, Pallas kernels, ffn_backward(): pl.pallas_call(kernel, grid=(2 * chunks,), in_specs=in_specs, out_specs=o...  78.2 us
    pallas_call x1, Pallas kernels, attention_forward(): pl.pallas_call(kernel, grid=(docs, pairs), in_specs=[block(0), block(1),...  15.2 us
    dot_general x1, matrix products, on_device_fast(): jnp.dot(hidden_low, up_weight, preferred_element_type=jnp.float32)  12.9 us
    dot_general x1, matrix products, on_device_fast(): jnp.dot(token_rows, qkv_weight, preferred_element_type=jnp.float32)  8.4 us
    dot_general x1, matrix products, on_device_fast(): jnp.dot(active, down_weight, preferred_element_type=jnp.float32)  5.47 us
    unnamed x65, local copies, waits for them, and re-layouts  5.03 us

commit v1 on v0

--- a/solution.py
+++ b/solution.py
@@ -76,10 +76,11 @@
 
 
 class Halving:
-    def __init__(self, place, names, order, source, own, received, send_sems, recv_sems, first_sem):
+    def __init__(self, place, names, order, source, own, received, send_sems, recv_sems, first_sem, tail=()):
         self.place, self.names, self.order = place, names, order
         self.source, self.own, self.received = source, own, received
-        self.send_sems, self.recv_sems, self.first_sem = send_sems, recv_sems, first_sem
+        self.last = True
+        self.send_sems, self.recv_sems, self.first_sem, self.tail = send_sems, recv_sems, first_sem, tail
 
     def region(self, step, mine):
         index = []
@@ -90,7 +91,7 @@
                 index.append(self.place.bit[name] if mine else 1 - self.place.bit[name])
             else:
                 index.append(slice(None))
-        return tuple(index)
+        return tuple(index) + self.tail
 
     def copy(self, step):
         held = self.source if step == 0 else self.own
@@ -109,15 +110,14 @@
     def add(self, step):
         self.copy(step).wait_recv()
         mine = self.region(step, True)
-        if step + 1 < len(self.order):
+        if step + 1 < len(self.order) or not self.last:
             self.own[mine] = self.own[mine] + self.received[step][...]
             return None
         return self.own[mine].astype(jnp.float32) + self.received[step][...].astype(jnp.float32)
 
     def merge(self, step):
-        self.copy(step).wait_recv()
-        mine = self.region(step, True)
-        self.own[mine] = self.own[mine] + self.received[step][...]
+        self.last = False
+        self.add(step)
 
     def close(self):
         for step in range(len(self.order)):
@@ -131,44 +131,136 @@
     return [core + narrow + x + near + far, core + x + near + narrow + far, core + near + narrow + x + far]
 
 
-def attention_forward(qkv, key_bias, docs, length):
-    width = qkv.shape[1] // 3
+def attention_forward(lengths, tokens, qkv_weight, vectors):
+    rows, width = tokens.shape
+    docs = lengths.shape[0]
+    length = rows // docs
     pairs = width // 128
 
-    def kernel(q_ref, k_ref, v_ref, bias_ref, mixed_ref, total_ref):
-        lane = lax.broadcasted_iota(jnp.int32, (1, 128), 1)
-        keys, values = k_ref[...], v_ref[...]
-        queries = q_ref[...] * jnp.bfloat16(HEAD_DIM**-0.5)
-        results = []
-        for head in range(2):
-            inside = (lane // HEAD_DIM) == head
-            masked = jnp.where(inside, queries, jnp.zeros_like(queries))
-            scores = dot_last(masked, keys) + bias_ref[0]
-            highest = jnp.max(scores, -1, keepdims=True)
-            powers = jnp.exp(scores - highest)
-            summed = jnp.sum(powers, -1, keepdims=True)
-            out = jnp.dot(powers.astype(jnp.bfloat16), values, preferred_element_type=jnp.float32)
-            results.append((out / summed, highest + jnp.log(summed)))
-        first = lane < HEAD_DIM
-        mixed_ref[...] = jnp.where(first, results[0][0], results[1][0]).astype(jnp.bfloat16)
-        total_ref[...] = jnp.where(first, results[0][1], results[1][1])
-
-    def block(which):
-        return pl.BlockSpec((length, 128), lambda doc, pair: (doc, which * pairs + pair))
-
-    rows = docs * length
+    def kernel(lens, tok, wq, wk, wv, vec, q_out, k_out, v_out, attention_out, mixed_out):
+        weights = jnp.concatenate([wq[...], wk[...], wv[...]], axis=1)
+        at = pl.ds(pl.multiple_of(pl.program_id(0) * 128, 128), 128)
+        offsets = jnp.concatenate([vec[6:7, at], jnp.zeros((1, 128), jnp.float32), vec[7:8, at]], axis=1)
+        qkv = (jnp.dot(tok[...], weights, preferred_element_type=jnp.float32) + offsets).astype(jnp.bfloat16)
+        q_out[...] = qkv[:, :128]
+        k_out[...] = qkv[:, 128:256]
+        v_out[...] = qkv[:, 256:]
+        first = lax.broadcasted_iota(jnp.int32, (1, 128), 1) < HEAD_DIM
+        for doc in range(docs):
+            some = slice(doc * length, (doc + 1) * length)
+            queries = qkv[some, :128] * jnp.bfloat16(HEAD_DIM**-0.5)
+            keys, values = qkv[some, 128:256], qkv[some, 256:]
+            zero = jnp.zeros_like(queries)
+            places = lax.broadcasted_iota(jnp.int32, (1, length), 1)
+            bias = jnp.where(places < lens[doc], 0.0, MASKED)
+            outs = []
+            for head in range(2):
+                masked = jnp.where(first, queries, zero) if head == 0 else jnp.where(first, zero, queries)
+                scores = dot_last(masked, keys) + bias
+                powers = jnp.exp(scores - jnp.max(scores, -1, keepdims=True))
+                attention = (powers * (1.0 / jnp.sum(powers, -1, keepdims=True))).astype(jnp.bfloat16)
+                attention_out[doc, head] = attention
+                outs.append(jnp.dot(attention, values, preferred_element_type=jnp.float32))
+            mixed_out[some, :] = jnp.where(first, outs[0], outs[1]).astype(jnp.bfloat16)
+
+    def whole(shape):
+        return pl.BlockSpec(shape, lambda pair: (0,) * len(shape), pipeline_mode=pl.Buffered(1))
+
+    column = pl.BlockSpec((rows, 128), lambda pair: (0, pair))
+    in_specs = [pl.BlockSpec(memory_space=pltpu.SMEM), whole((rows, width))]
+    in_specs += [pl.BlockSpec((width, 128), lambda pair, n=n: (0, n * pairs + pair)) for n in range(3)]
+    in_specs += [whole(vectors.shape)]
+    low = jax.ShapeDtypeStruct((rows, width), jnp.bfloat16)
     return pl.pallas_call(
         kernel,
-        grid=(docs, pairs),
-        in_specs=[block(0), block(1), block(2), pl.BlockSpec((1, 1, length), lambda doc, pair: (doc, 0, 0))],
-        out_specs=[block(0), block(0)],
-        out_shape=[
-            jax.ShapeDtypeStruct((rows, width), jnp.bfloat16),
-            jax.ShapeDtypeStruct((rows, width), jnp.float32),
+        grid=(pairs,),
+        in_specs=in_specs,
+        out_specs=[column] * 3
+        + [pl.BlockSpec((docs, 2, length, length), lambda pair: (0, pair, 0, 0)), column],
+        out_shape=[low] * 3 + [jax.ShapeDtypeStruct((docs, 2 * pairs, length, length), jnp.bfloat16), low],
+        compiler_params=pltpu.CompilerParams(vmem_limit_bytes=56 << 20),
+        name="attention_forward",
+    )(lengths, tokens, qkv_weight, qkv_weight, qkv_weight, vectors)
+
+
+def ffn_forward(lengths, mixed, tokens, out_weight, vectors, up_weight, down_weight):
+    rows, width = tokens.shape
+    ff = up_weight.shape[1]
+    chunk = width
+    chunks = ff // chunk
+    length = rows // lengths.shape[0]
+    row_block = 128
+
+    def kernel(lens, mix, tok, ow, vec, up, down, hid_out, n1_out, q1_out, act_out, slope_out, n2_out, q2_out,
+               enc_out, hidden, total):
+        pid = pl.program_id(0)
+
+        def each_block(body):
+            def step(i, carry):
+                body(pl.multiple_of(i * row_block, row_block))
+                return carry
+
+            lax.fori_loop(0, rows // row_block, step, 0)
+
+        @pl.when(pid == 0)
+        def _():
+            total[...] = jnp.dot(mix[...], ow[...], preferred_element_type=jnp.float32)
+
+            def body(at):
+                some = pl.ds(at, row_block)
+                summed = tok[some, :].astype(jnp.float32) + (total[some, :] + vec[0:1, :])
+                out, normed, inverse = norm_forward(summed, vec[1:2, :], vec[2:3, :])
+                hidden[some, :] = out
+                hid_out[some, :] = out.astype(jnp.bfloat16)
+                n1_out[some, :] = normed.astype(jnp.bfloat16)
+                q1_out[some, :] = inverse
+                total[some, :] = jnp.zeros_like(out)
+
+            each_block(body)
+
+        pre = jnp.dot(hid_out[...], up[...], preferred_element_type=jnp.float32) + vec[pl.ds(pid + 9, 1), :]
+        cumulative = normal_cdf(pre)
+        density = jnp.exp(-0.5 * pre * pre) * 0.3989422804014327
+        active = (pre * cumulative).astype(jnp.bfloat16)
+        act_out[...] = active
+        slope_out[...] = (cumulative + pre * density).astype(jnp.bfloat16)
+        total[...] += jnp.dot(active, down[...], preferred_element_type=jnp.float32)
+
+        @pl.when(pid == chunks - 1)
+        def _():
+            def body(at):
+                some = pl.ds(at, row_block)
+                summed = hidden[some, :] + (total[some, :] + vec[3:4, :])
+                out, normed, inverse = norm_forward(summed, vec[4:5, :], vec[5:6, :])
+                n2_out[some, :] = normed.astype(jnp.bfloat16)
+                q2_out[some, :] = inverse
+                doc = at // length
+                line = lax.broadcasted_iota(jnp.int32, (row_block, 1), 0) + (at - doc * length)
+                enc_out[some, :] = jnp.where(line < lens[doc], out, 0.0).astype(jnp.bfloat16)
+
+            each_block(body)
+
+    def whole(shape):
+        return pl.BlockSpec(shape, lambda f: (0,) * len(shape), pipeline_mode=pl.Buffered(1))
+
+    wide_row, column = whole((rows, width)), pl.BlockSpec((rows, chunk), lambda f: (0, f))
+    low = jax.ShapeDtypeStruct((rows, width), jnp.bfloat16)
+    one = jax.ShapeDtypeStruct((rows, 1), jnp.float32)
+    upper = jax.ShapeDtypeStruct((rows, ff), jnp.bfloat16)
+    return pl.pallas_call(
+        kernel,
+        grid=(chunks,),
+        in_specs=[
+            pl.BlockSpec(memory_space=pltpu.SMEM), wide_row, wide_row, whole((width, width)), whole(vectors.shape),
+            pl.BlockSpec((width, chunk), lambda f: (0, f)),
+            pl.BlockSpec((chunk, width), lambda f: (f, 0)),
         ],
-        compiler_params=pltpu.CompilerParams(vmem_limit_bytes=48 << 20),
-        name="attention_forward",
-    )(qkv, qkv, qkv, key_bias)
+        out_specs=[wide_row, wide_row, whole((rows, 1)), column, column, wide_row, whole((rows, 1)), wide_row],
+        out_shape=[low, low, one, upper, upper, low, one, low],
+        scratch_shapes=[pltpu.VMEM((rows, width), jnp.float32), pltpu.VMEM((rows, width), jnp.float32)],
+        compiler_params=pltpu.CompilerParams(vmem_limit_bytes=58 << 20),
+        name="ffn_forward",
+    )(lengths, mixed, tokens, out_weight, vectors, up_weight, down_weight)
 
 
 def dot_last(left, right):
@@ -196,11 +288,11 @@
     return jnp.where(lines == row, 1.0, 0.0).astype(jnp.bfloat16)
 
 
-def ffn_backward(lengths, numbers, encoded, cotangent, dir_rows, dir_bias, normed_two, inverse_two, second_gain, active, slope, hidden_low, down_weight, up_weight,
-                 normed_one, inverse_one, first_gain):
+def ffn_backward(lengths, numbers, encoded, cotangent, dir_t, vectors, normed_two, inverse_two, active, slope, hidden_low, down_weight, up_weight,
+                 normed_one, inverse_one):
     rows, width = hidden_low.shape
     ff = active.shape[1]
-    segments, classes = numbers.shape[1], dir_bias.shape[0]
+    segments, classes = numbers.shape[1], dir_t.shape[0]
     length = rows // lengths.shape[0]
     names = axis_bits()
     steps = len(names)
@@ -213,6 +305,7 @@
     row_steps = rows // row_block
     orders = link_orders()
     two = (2,)
+    early = 3
     first_dir = 6 + narrow
     sum_rows = pl.cdiv(first_dir + 3 * classes, 8) * 8
 
@@ -224,34 +317,35 @@
         return tuple((number >> bit) & 1 for bit in reversed(range(count)))
 
     def kernel(*refs):
-        lens, nums, enc, cot, dir_w, dir_b = refs[:6]
-        refs = refs[6:]
-        (n2, q2, gain2, n1, q1, gain1, hidden) = refs[:7]
-        refs = refs[7:]
-        act = refs[:narrow]
-        slo = refs[narrow : 2 * narrow]
-        dws = refs[2 * narrow : 3 * narrow]
-        uws = refs[3 * narrow : 4 * narrow]
-        rest = list(refs[4 * narrow :])
+        lens, nums, enc, cot, dir_ref = refs[:5]
+        refs = refs[5:]
+        q2, q1, vec = refs[:3]
+        far = refs[3:9]
+        slo = refs[9 : 9 + narrow]
+        rest = list(refs[9 + narrow :])
         ga_out, up_out, down_out, sums_out = rest[:4]
         rest = rest[4:]
         grad_hidden, lowered, lowered_t, hidden_t, own, up_own, up_received = rest[:7]
-        received = rest[7 : 7 + steps]
-        select, leaving, arrived, leaving_grads, arrived_grads = rest[7 + steps : 12 + steps]
-        send_sems, recv_sems, local_sems = rest[12 + steps :]
+        received = rest[7 : 7 + early]
+        rest = rest[7 + early :]
+        select, picked, dir_w, leaving, arrived, leaving_grads, arrived_grads = rest[:7]
+        near = rest[7:13]
+        n2, hidden, act, dws, uws, n1 = near
+        send_sems, recv_sems, local_sems = rest[13:]
+        loads = [pltpu.make_async_copy(far[i], near[i], local_sems.at[2 * chunks + i]) for i in range(len(near))]
         pid = pl.program_id(0)
         place = Place()
         pieces = []
         for number in range(chunks):
             pieces.append(
-                Halving(place, names, orders[number % 3], own.at[number], own.at[number],
-                        [r.at[number] for r in received], send_sems, recv_sems, number * steps)
+                Halving(place, names, orders[number % 3][:early], own.at[number], own.at[number],
+                        [r.at[number] for r in received], send_sems, recv_sems, number * early)
             )
         core = ("narrow", 0)
         up_names = [name for name in names if name != ("wide", 0)]
         up_pieces = [
             Halving(place, up_names, [core], up_own.at[number], up_own.at[number], [up_received.at[number]],
-                    send_sems, recv_sems, chunks * steps + number)
+                    send_sems, recv_sems, chunks * early + number)
             for number in range(chunks)
         ]
 
@@ -277,44 +371,56 @@
             landing[me] = source[me]
             for copy in made:
                 copy.wait()
-            return landing[...].reshape(segments, width)
+            return landing[...].reshape(segments, 128)
 
         @pl.when(pid == 0)
         def _():
+            for load in loads:
+                load.start()
             place.greet(all_wide=True)
             sums_out[...] = jnp.zeros_like(sums_out)
-            base = chunks * steps + chunks
+            base = chunks * early + chunks
             select[...] = dot_last(one_hot(nums[0:1, :], rows), one_hot(nums[1:2, :], segments)).astype(jnp.bfloat16)
-            picked = jnp.dot(select[...].T, enc[...], preferred_element_type=jnp.float32).astype(jnp.bfloat16)
-            leaving[...] = picked.reshape(leaving.shape)
-            rows_in = exchange(leaving, arrived, base)
+            picked[...] = jnp.dot(select[...].T, enc[...], preferred_element_type=jnp.float32).astype(jnp.bfloat16)
+            halves = [dir_ref[:, n * width : (n + 1) * width].astype(jnp.float32) for n in range(2)]
+            blank = jnp.zeros((128 - 2 * classes, width), jnp.float32)
+            dir_w[...] = jnp.concatenate(halves + [blank]).astype(jnp.bfloat16)
+            leaving[...] = dot_last(picked[...], dir_w[...]).reshape(leaving.shape)
+            scores = exchange(leaving, arrived, base).T
             pair_first, pair_second = one_hot(nums[2:3, :], segments), one_hot(nums[3:4, :], segments)
-            scores = dot_last(dir_w[...], rows_in)
 
             def chosen(values, pairs):
                 split = jnp.dot(parts_of(values, 3), pairs, preferred_element_type=jnp.float32)
                 return split[:classes] + split[classes : 2 * classes] + split[2 * classes :]
 
-            logits = chosen(scores[:classes], pair_first) + chosen(scores[classes:], pair_second) + dir_b[...]
+            logits = chosen(scores[:classes], pair_first) + chosen(scores[classes : 2 * classes], pair_second)
+            logits = logits + jnp.broadcast_to(vec[8:9, :128], (128, 128)).T[:classes, 0:1]
             powers = jnp.exp(logits - jnp.max(logits, 0, keepdims=True))
             chance = powers / jnp.sum(powers, 0, keepdims=True)
             kinds = lax.broadcasted_iota(jnp.int32, logits.shape, 0)
             delta = chance - jnp.where(kinds == nums[4:5, :], 1.0, 0.0)
-            sums_out[first_dir + 2 * classes : first_dir + 3 * classes, :] = jnp.broadcast_to(
-                jnp.sum(delta, 1, keepdims=True), (classes, width)
-            )
             split = parts_of(delta, 2)
             gathered = []
             for pairs in (pair_first, pair_second):
                 both = dot_last(split, pairs)
                 gathered.append(both[:classes] + both[classes:])
-            per_row = parts_of(jnp.concatenate(gathered), 2)
-            both = jnp.dot(per_row, rows_in, preferred_element_type=jnp.float32)
+            gathered.append(jnp.zeros((128 - 2 * classes, segments), jnp.float32))
+            leaving_grads[...] = jnp.concatenate(gathered).T.reshape(leaving.shape)
+            sums_out[first_dir + 2 * classes : first_dir + 3 * classes, :] = jnp.broadcast_to(
+                jnp.sum(delta, 1, keepdims=True), (classes, width)
+            )
+            back = exchange(leaving_grads, arrived_grads, base + wide - 1)
+            coarse = back.astype(jnp.bfloat16)
+            fine = (back - coarse.astype(jnp.float32)).astype(jnp.bfloat16)
+            grads_in = (
+                jnp.dot(coarse, dir_w[...], preferred_element_type=jnp.float32)
+                + jnp.dot(fine, dir_w[...], preferred_element_type=jnp.float32)
+            ).astype(jnp.bfloat16)
+            back_t = back.T[: 2 * classes]
+            both = jnp.dot(parts_of(back_t, 2), picked[...], preferred_element_type=jnp.float32)
             sums_out[first_dir : first_dir + 2 * classes, :] = both[: 2 * classes] + both[2 * classes :]
-            twice = jnp.concatenate([dir_w[...], dir_w[...]])
-            grads = jnp.dot(per_row.T, twice, preferred_element_type=jnp.float32).astype(jnp.bfloat16)
-            leaving_grads[...] = grads.reshape(leaving.shape)
-            grads_in = exchange(leaving_grads, arrived_grads, base + wide - 1)
+            loads[0].wait()
+            loads[1].wait()
 
             def body(i, carry):
                 at = pl.multiple_of(i * row_block, row_block)
@@ -326,7 +432,7 @@
                     select[some, :], grads_in, preferred_element_type=jnp.float32
                 )
                 grad = jnp.where(line < lens[doc], grad, 0.0)
-                two = norm_back_rows(grad, normed, q2[some, :], gain2[...])
+                two = norm_back_rows(grad, normed, q2[some, :], vec[4:5, :])
                 low = two.astype(jnp.bfloat16)
                 grad_hidden[some, :] = two
                 lowered[some, :] = low
@@ -339,9 +445,16 @@
 
             lax.fori_loop(0, row_steps, body, 0)
 
+        def slab(n, step):
+            return pl.ds(pl.multiple_of((n * chunks + chunk_of(step)) * 128, 128), 128)
+
+        @pl.when(pid == 0)
+        def _():
+            loads[2].wait()
+
         @pl.when(pid < chunks)
         def _():
-            actives = jnp.concatenate([ref[...] for ref in act], axis=1)
+            actives = jnp.concatenate([act[:, slab(n, pid)] for n in range(narrow)], axis=1)
             result = jnp.dot(lowered_t[...], actives, preferred_element_type=jnp.float32).astype(jnp.bfloat16)
             for w in range(wide):
                 for n in range(narrow):
@@ -349,11 +462,16 @@
                         w * d_rows : (w + 1) * d_rows, n * 128 : (n + 1) * 128
                     ]
 
+        @pl.when(pid == chunks)
+        def _():
+            for load in loads[3:]:
+                load.wait()
+
         @pl.when(pid >= chunks)
         def _():
             slopes = jnp.concatenate([ref[...] for ref in slo], axis=1)
-            downs = jnp.concatenate([ref[...] for ref in dws], axis=0)
-            ups = jnp.concatenate([ref[...] for ref in uws], axis=1)
+            downs = jnp.concatenate([dws[slab(n, pid - chunks), :] for n in range(narrow)], axis=0)
+            ups = jnp.concatenate([uws[:, slab(n, pid - chunks)] for n in range(narrow)], axis=1)
             grad_active = dot_last(lowered[...], downs)
             grad_upper = (grad_active * slopes.astype(jnp.float32)).astype(jnp.bfloat16)
             totals = jnp.sum(grad_upper.astype(jnp.float32), 0, keepdims=True)
@@ -369,14 +487,17 @@
                     ]
             grad_hidden[...] += dot_last(grad_upper, ups)
 
+        def down_write(number):
+            return pltpu.make_async_copy(
+                own.at[number].at[pieces[number].region(early - 1, True)], down_out.at[number], local_sems.at[chunks + number]
+            )
+
         def advance(number, step):
-            item = pieces[number]
-            total = item.add(step)
-            if total is None:
-                item.send(step + 1)
+            pieces[number].merge(step)
+            if step + 1 < early:
+                pieces[number].send(step + 1)
             else:
-                j = number // 2 + third * (number % 2)
-                down_out[:, j * 128 : (j + 1) * 128] = total
+                down_write(number).start()
 
         for number in range(chunks):
             @pl.when(pid == chunks + number)
@@ -389,7 +510,7 @@
                 at = pl.multiple_of(i * row_block, row_block)
                 some = pl.ds(at, row_block)
                 grad, normed = grad_hidden[some, :], n1[some, :].astype(jnp.float32)
-                low = norm_back_rows(grad, normed, q1[some, :], gain1[...]).astype(jnp.bfloat16)
+                low = norm_back_rows(grad, normed, q1[some, :], vec[1:2, :]).astype(jnp.bfloat16)
                 ga_out[some, :] = low
                 sums_out[3:4, :] += jnp.sum(grad * normed, 0, keepdims=True)
                 sums_out[4:5, :] += jnp.sum(grad, 0, keepdims=True)
@@ -400,8 +521,8 @@
 
         plan = {}
         for number in range(chunks):
-            for step in range(steps):
-                at = number + 1 if step == 0 else chunks + number // 2 + step
+            for step in range(early):
+                at = (number + 1, chunks + 1 + 2 * (number // 3), chunks + 4 + number // 3)[step]
                 plan.setdefault(min(at, 2 * chunks - 1), []).append((step, number))
         for at in range(2 * chunks):
             @pl.when(pid == at)
@@ -418,6 +539,7 @@
                     up_write(chunks - 1).start()
                     for number in range(chunks):
                         up_write(number).wait()
+                        down_write(number).wait()
                     for item in pieces + up_pieces:
                         item.close()
 
@@ -428,25 +550,22 @@
         return [pl.BlockSpec(shape, lambda g, n=n: (0, n * chunks + chunk_of(g - first))) for n in range(narrow)]
 
     in_specs = [pl.BlockSpec(memory_space=pltpu.SMEM), whole(numbers.shape), whole((rows, width)), whole((rows, width))]
-    in_specs += [whole(dir_rows.shape), whole(dir_bias.shape)]
-    in_specs += [whole((rows, width)), whole((rows, 1)), whole((1, width))]
-    in_specs += [whole((rows, width)), whole((rows, 1)), whole((1, width)), whole((rows, width))]
-    in_specs += slab_columns((rows, 128), 0) + slab_columns((rows, 128), chunks)
-    in_specs += [pl.BlockSpec((128, width), lambda g, n=n: (n * chunks + chunk_of(g - chunks), 0)) for n in range(narrow)]
-    in_specs += slab_columns((width, 128), chunks)
+    in_specs += [whole(dir_t.shape)]
+    in_specs += [whole((rows, 1))] * 2 + [whole(vectors.shape)] + [pl.BlockSpec(memory_space=pl.ANY)] * 6
+    in_specs += slab_columns((rows, 128), chunks)
     high = two * (wide_bits - 1)
     low = two * narrow_bits
     up_shape = (third,) + high + (2,) + low[1:] + (u_rows, 128)
     out_specs = [
         whole((rows, width)),
         pl.BlockSpec(memory_space=pl.ANY),
-        whole((d_rows, chunks * 128)),
+        pl.BlockSpec(memory_space=pl.ANY),
         whole((sum_rows, width)),
     ]
     out_shape = [
         jax.ShapeDtypeStruct((rows, width), jnp.bfloat16),
         jax.ShapeDtypeStruct(up_shape, jnp.bfloat16),
-        jax.ShapeDtypeStruct((d_rows, chunks * 128), jnp.float32),
+        jax.ShapeDtypeStruct((chunks,) + two * (steps - early) + (d_rows, 128), jnp.bfloat16),
         jax.ShapeDtypeStruct((sum_rows, width), jnp.float32),
     ]
     scratch = [
@@ -458,11 +577,14 @@
         pltpu.VMEM((chunks,) + high + low + (u_rows, 128), jnp.bfloat16),
         pltpu.VMEM((chunks,) + high + low[1:] + (u_rows, 128), jnp.bfloat16),
     ]
-    scratch += [pltpu.VMEM((chunks,) + two * (steps - 1 - s) + (d_rows, 128), jnp.bfloat16) for s in range(steps)]
-    scratch += [pltpu.VMEM((rows, segments), jnp.bfloat16)]
-    scratch += [pltpu.VMEM((wide, segments // wide, width), jnp.bfloat16)] * 4
-    sems = chunks * steps + chunks + 2 * (wide - 1)
-    scratch += [pltpu.SemaphoreType.DMA((sems,)), pltpu.SemaphoreType.DMA((sems,)), pltpu.SemaphoreType.DMA((chunks,))]
+    scratch += [pltpu.VMEM((chunks,) + two * (steps - 1 - s) + (d_rows, 128), jnp.bfloat16) for s in range(early)]
+    scratch += [pltpu.VMEM((rows, segments), jnp.bfloat16), pltpu.VMEM((segments, width), jnp.bfloat16)]
+    scratch += [pltpu.VMEM((128, width), jnp.bfloat16)]
+    scratch += [pltpu.VMEM((wide, segments // wide, 128), jnp.float32)] * 4
+    far = (normed_two, hidden_low, active, down_weight, up_weight, normed_one)
+    scratch += [pltpu.VMEM(item.shape, item.dtype) for item in far]
+    sems = chunks * early + chunks + 2 * (wide - 1)
+    scratch += [pltpu.SemaphoreType.DMA((sems,)), pltpu.SemaphoreType.DMA((sems,)), pltpu.SemaphoreType.DMA((2 * chunks + len(far),))]
     return pl.pallas_call(
         kernel,
         grid=(2 * chunks,),
@@ -470,15 +592,16 @@
         out_specs=out_specs,
         out_shape=out_shape,
         scratch_shapes=scratch,
-        compiler_params=pltpu.CompilerParams(collective_id=0, has_side_effects=True, vmem_limit_bytes=58 << 20),
+        compiler_params=pltpu.CompilerParams(collective_id=0, has_side_effects=True, vmem_limit_bytes=60 << 20),
         name="ffn_backward",
-    )(lengths, numbers, encoded, cotangent, dir_rows, dir_bias, normed_two, inverse_two, second_gain, normed_one, inverse_one, first_gain, hidden_low,
-      *([active] * narrow), *([slope] * narrow), *([down_weight] * narrow), *([up_weight] * narrow))
-
-
-def attention_backward(grad_attended, mixed, out_weight, qkv, totals, key_bias, tokens, qkv_weight, up_grads, sums):
+    )(lengths, numbers, encoded, cotangent, dir_t, inverse_two, inverse_one, vectors,
+      *far, *([slope] * narrow))
+
+
+def attention_backward(grad_attended, mixed, out_weight, queries, keys, values, attention, tokens, qkv_weight, up_grads,
+                       down_grads, sums):
     rows, width = tokens.shape
-    docs, _, length = key_bias.shape
+    docs, _, length, _ = attention.shape
     pairs = width // 128
     names = axis_bits()
     steps = len(names)
@@ -498,33 +621,55 @@
     first_q = 1 + attn_steps
     first_t = first_q + q_parts
     grid = first_t + token_steps
-    count = ups + 1 + q_parts
+    downs, d_rows = down_grads.shape[0], down_grads.shape[-2]
+    down_steps = len(down_grads.shape) - 3
+    cuts = [(0, q_rows // 32 * 16), (q_rows // 32 * 16, q_rows)]
+    u_cuts = [(0, u_rows // 2), (u_rows // 2, u_rows)]
+    up_count, out_count = ups * len(u_cuts), q_parts
+    first_part = up_count + out_count
+    first_down = first_part + q_parts * len(cuts)
+    count = first_down + downs
     small_rows = sums.shape[0]
 
     def bits_of(number, count):
         return tuple((number >> bit) & 1 for bit in reversed(range(count)))
 
     def kernel(*refs):
-        (ga, mix, ow, q_ref, k_ref, v_ref, tot_ref, bias, tok_hbm, qw_hbm, up_hbm, small) = refs[:12]
-        tokens_out, up_out, out_out, qkv_out, small_out, late_out = refs[12:18]
-        rest = list(refs[18:])
+        (ga_hbm, mix_hbm, ow_hbm, q_ref, k_ref, v_ref, att_ref, tok_hbm, qw_hbm, up_hbm, down_hbm, small) = refs[:12]
+        tokens_out, up_out, out_out, qkv_out, down_out, small_out, late_out = refs[12:19]
+        rest = list(refs[19:])
         gm, mix_pair, gqkv_t, up_own, out_own, qkv_own = rest[:6]
         rest = rest[6:]
-        up_received, rest = rest[: steps - 1], rest[steps - 1 :]
-        out_received, qkv_received, rest = rest[:steps], rest[steps : 2 * steps], rest[2 * steps :]
-        small_sent, small_received, late_sent, late_received, swap_out, swap_qkv, tok, qw = rest[:8]
-        send_sems, recv_sems, local_sems = rest[8:]
+        up_received = [rest[i * (steps - 1) : (i + 1) * (steps - 1)] for i in range(len(u_cuts))]
+        rest = rest[len(u_cuts) * (steps - 1) :]
+        out_received, rest = rest[:steps], rest[steps:]
+        qkv_received, rest = [rest[i * steps : (i + 1) * steps] for i in range(len(cuts))], rest[len(cuts) * steps :]
+        down_own, down_received, rest = rest[0], rest[1 : 1 + down_steps], rest[1 + down_steps :]
+        small_sent, small_received, late_sent, late_received, swap_out, swap_qkv, tok, qw, ga, mix, ow = rest[:11]
+        send_sems, recv_sems, local_sems = rest[11:]
         pid = pl.program_id(0)
         place = Place()
         core = place.bit["narrow", 0]
         pieces = []
-        for number in range(ups):
-            pieces.append(Halving(place, names[:-1], orders[number % 3][1:], up_hbm.at[number], up_own.at[number],
-                                  [r.at[number] for r in up_received], send_sems, recv_sems, number * steps))
-        pieces.append(Halving(place, names, orders[1], out_own, out_own, out_received, send_sems, recv_sems, ups * steps))
-        for number in range(q_parts):
-            pieces.append(Halving(place, names, orders[number % 3], qkv_own.at[number], qkv_own.at[number],
-                                  [r.at[number] for r in qkv_received], send_sems, recv_sems, (ups + 1 + number) * steps))
+        for low, high in u_cuts:
+            for part in range(ups):
+                cut = len(pieces) // ups
+                pieces.append(Halving(place, names[:-1], orders[part % 3][1:], up_hbm.at[part], up_own.at[part],
+                                      [r.at[part] for r in up_received[cut]], send_sems, recv_sems, len(pieces) * steps,
+                                      (slice(low, high), slice(None))))
+        for part in range(out_count):
+            pieces.append(Halving(place, names, orders[part % 3], out_own.at[part], out_own.at[part],
+                                  [r.at[part] for r in out_received], send_sems, recv_sems, len(pieces) * steps))
+        for part in range(q_parts):
+            for cut, (low, high) in enumerate(cuts):
+                pieces.append(Halving(place, names, orders[part % 3], qkv_own.at[part], qkv_own.at[part],
+                                      [r.at[part] for r in qkv_received[cut]], send_sems, recv_sems, len(pieces) * steps,
+                                      (slice(low, high), slice(None))))
+        for number in range(downs):
+            order = orders[number % 3][steps - down_steps :]
+            pieces.append(Halving(place, [name for name in names if name in order], order, down_own.at[number],
+                                  down_own.at[number], [r.at[number] for r in down_received], send_sems, recv_sems,
+                                  len(pieces) * steps))
         base = count * steps
 
         def all_sum(sent, received, first):
@@ -538,18 +683,22 @@
 
         small_copies = all_sum(small_sent, small_received, base)
         late_copies = all_sum(late_sent, late_received, base + steps)
-        swap_refs = [swap_out.at[core]] + [swap_qkv.at[number, core] for number in range(q_parts)]
+        swap_refs = [swap_out.at[part, core] for part in range(out_count)]
+        swap_refs += [swap_qkv.at[part, core, low:high] for part in range(q_parts) for low, high in cuts]
         swaps = [pltpu.make_async_remote_copy(
             src_ref=ref, dst_ref=ref, send_sem=send_sems.at[base + 2 * steps + slot],
             recv_sem=recv_sems.at[base + 2 * steps + slot], device_id=place.across(("narrow", 0)),
             device_id_type=MESH_ID) for slot, ref in enumerate(swap_refs)]
         local = []
         for number in range(ups):
-            keep = pieces[number].region(0, True)
+            keep = pieces[number].region(0, True)[: -2]
             local.append(pltpu.make_async_copy(up_hbm.at[number].at[keep], up_own.at[number].at[keep], local_sems.at[number]))
 
         loads = [pltpu.make_async_copy(tok_hbm, tok, local_sems.at[ups]),
                  pltpu.make_async_copy(qw_hbm, qw, local_sems.at[ups + 1])]
+        first_loads = [pltpu.make_async_copy(source, target, local_sems.at[ups + 3 + i])
+                       for i, (source, target) in enumerate(((ga_hbm, ga), (mix_hbm, mix), (ow_hbm, ow)))]
+        down_load = pltpu.make_async_copy(down_hbm, down_own, local_sems.at[ups + 2])
 
         def advance(number, step):
             item = pieces[number]
@@ -558,14 +707,20 @@
             total = item.add(step)
             if total is None:
                 item.send(step + 1)
-            elif number < ups:
-                up_out[:, number * 128 : (number + 1) * 128] = total
+            elif number < up_count:
+                cut, part = divmod(number, ups)
+                up_out[u_cuts[cut][0] : u_cuts[cut][1], part * 128 : (part + 1) * 128] = total
+            elif number >= first_down:
+                number -= first_down
+                j = number // 2 + downs // 2 * (number % 2)
+                down_out[:, j * 128 : (j + 1) * 128] = total
             else:
-                if number == ups:
-                    swap_out[core] = total
+                if number < first_part:
+                    swap_out[number - up_count, core] = total
                 else:
-                    swap_qkv[number - ups - 1, core] = total
-                swaps[number - ups].start()
+                    part, cut = divmod(number - first_part, len(cuts))
+                    swap_qkv[part, core, cuts[cut][0] : cuts[cut][1]] = total
+                swaps[number - up_count].start()
 
         def advance_small(copies, sent, received, out, step):
             copies[step].wait_recv()
@@ -579,27 +734,39 @@
         @pl.when(pid == 0)
         def _():
             place.greet()
+            for number in range(up_count):
+                pieces[number].send(0)
             for number in range(ups):
-                pieces[number].send(0)
                 local[number].start()
+            for load in first_loads:
+                load.start()
             small_sent[0] = small[...]
             small_copies[0].start()
+            down_load.start()
             for load in loads:
                 load.start()
+            for load in first_loads:
+                load.wait()
             grads_t = ga[...].T
             result = jnp.dot(grads_t, mix[...], preferred_element_type=jnp.float32).astype(jnp.bfloat16)
             for w in range(wide):
                 for h in range(2):
                     for y in range(half):
                         at = (w * 2 + h) * o_rows
-                        out_own[bits_of(w, wide_bits) + bits_of(y, half_bits) + (h,)] = result[
-                            at : at + o_rows, y * lanes : (y + 1) * lanes
-                        ]
-            pieces[ups].send(0)
+                        for part in range(out_count):
+                            first = y * lanes + part * 128
+                            out_own[(part,) + bits_of(w, wide_bits) + bits_of(y, half_bits) + (h,)] = result[
+                                at : at + o_rows, first : first + 128
+                            ]
+            for part in range(out_count):
+                pieces[up_count + part].send(0)
             grad_mixed = dot_last(ga[...], ow[...]).astype(jnp.bfloat16)
             for pair in range(pairs):
                 gm[pair] = grad_mixed[:, pair * 128 : (pair + 1) * 128]
                 mix_pair[pair] = mix[:, pair * 128 : (pair + 1) * 128]
+            down_load.wait()
+            for number in range(downs):
+                pieces[first_down + number].send(0)
 
         @pl.when((pid >= 1) & (pid < first_q))
         def _():
@@ -607,25 +774,22 @@
             pair, doc = number // docs, number % docs
             some = pl.ds(pl.multiple_of(doc * length, length), length)
             lane = lax.broadcasted_iota(jnp.int32, (1, 128), 1)
-            scale = jnp.bfloat16(HEAD_DIM**-0.5)
-            queries, keys, values = q_ref[...] * scale, k_ref[...], v_ref[...]
+            scaled, keys, values = q_ref[...] * jnp.bfloat16(HEAD_DIM**-0.5), k_ref[...], v_ref[...]
             grads = gm[pair, some, :]
             product = grads.astype(jnp.float32) * mix_pair[pair, some, :].astype(jnp.float32)
-            queries_t, grads_t = queries.T, grads.T
-            zero = jnp.zeros_like(queries)
+            queries_t, grads_t = scaled.T, grads.T
+            zero = jnp.zeros_like(grads)
             query_parts = []
             for head in range(2):
                 inside = (lane // HEAD_DIM) == head
                 at = head * HEAD_DIM
-                scores = dot_last(jnp.where(inside, queries, zero), keys) + bias[0]
-                attention = jnp.exp(scores - tot_ref[:, at : at + 1])
+                attention = att_ref[0, head]
                 chance = dot_last(jnp.where(inside, grads, zero), values)
                 inner = jnp.sum(jnp.where(inside, product, 0.0), -1, keepdims=True)
-                grad_scores = (attention * (chance - inner)).astype(jnp.bfloat16)
+                grad_scores = (attention.astype(jnp.float32) * (chance - inner)).astype(jnp.bfloat16)
                 query_parts.append(jnp.dot(grad_scores, keys, preferred_element_type=jnp.float32))
                 key_t = jnp.dot(queries_t[at : at + HEAD_DIM], grad_scores, preferred_element_type=jnp.float32)
-                value_t = jnp.dot(grads_t[at : at + HEAD_DIM], attention.astype(jnp.bfloat16),
-                                  preferred_element_type=jnp.float32)
+                value_t = jnp.dot(grads_t[at : at + HEAD_DIM], attention, preferred_element_type=jnp.float32)
                 row = pair * 128 + at
                 gqkv_t[pl.ds(pl.multiple_of(width + row, HEAD_DIM), HEAD_DIM), some] = key_t.astype(jnp.bfloat16)
                 gqkv_t[pl.ds(pl.multiple_of(2 * width + row, HEAD_DIM), HEAD_DIM), some] = value_t.astype(jnp.bfloat16)
@@ -654,42 +818,57 @@
                             qkv_own[(part,) + bits_of(w, wide_bits) + bits_of(y, half_bits) + (h,)] = result[
                                 at : at + q_rows, y * 128 : (y + 1) * 128
                             ]
-                pieces[ups + 1 + part].send(0)
+                for cut in range(len(cuts)):
+                    pieces[first_part + part * len(cuts) + cut].send(0)
 
         @pl.when(pid >= first_t)
         def _():
             at = pl.multiple_of((pid - first_t) * token_block, token_block)
             some = pl.ds(at, token_block)
             grad_t = jnp.dot(qw[...], gqkv_t[:, some], preferred_element_type=jnp.float32)
-            tokens_out[some, :] = (grad_t.T + ga[some, :].astype(jnp.float32)).astype(jnp.bfloat16)
+            tokens_out[...] = (grad_t.T + ga[some, :].astype(jnp.float32)).astype(jnp.bfloat16)
 
         plan, small_plan, late_plan = {}, {}, {}
-        for step, at in enumerate((4, 7, 8, 11)):
-            for number in range(ups):
+        for cut, times in enumerate(((4, 7, 9, 12), (6, 8, 10, 14))):
+            for step, at in enumerate(times):
+                for part in range(ups):
+                    plan.setdefault(at, []).append((cut * ups + part, step))
+        for step, at in enumerate((1, 8, 10, 12, 14)):
+            for part in range(out_count):
+                plan.setdefault(at, []).append((up_count + part, step))
+        for step, at in enumerate((3, 6)):
+            for number in range(downs):
+                plan.setdefault(at, []).append((first_down + number, step))
+        for number in range(first_part, first_down):
+            for step in range(steps):
+                at = first_q + (number - first_part) // len(cuts) + 1 if step == 0 else grid - 1
                 plan.setdefault(at, []).append((number, step))
-        for step, at in enumerate((1, 7, 9, 10, 12)):
-            plan.setdefault(at, []).append((ups, step))
-        for part in range(q_parts):
-            for step in range(steps):
-                plan.setdefault(first_q + part + 1 if step == 0 else grid - 1, []).append((ups + 1 + part, step))
-        for step, at in enumerate((2, 3, 5, 7, 9)):
+        for step, at in enumerate((3, 6, 8, 10, 12)):
             small_plan[at] = step
-        for step in range(steps):
-            late_plan[first_q + 1 + step] = step
+        late_plan[first_q + 2] = 0
         for at in range(grid):
             @pl.when(pid == at)
             def _():
                 if at in small_plan:
                     advance_small(small_copies, small_sent, small_received, small_out, small_plan[at])
                 for number, step in sorted(plan.get(at, []), key=lambda entry: (entry[1], entry[0])):
+                    if at == grid - 1 and number == first_part:
+                        advance_small(late_copies, late_sent, late_received, late_out, step)
                     advance(number, step)
                 if at in late_plan:
                     advance_small(late_copies, late_sent, late_received, late_out, late_plan[at])
                 if at == grid - 1:
                     for copy in swaps:
                         copy.wait()
-                    out_out[...] = swap_out[...]
-                    qkv_out[...] = swap_qkv[...]
+
+                    def own_lanes(lanes):
+                        size = lanes.shape[1] // 2
+                        return jnp.where(core == 0, lanes[:, :size], lanes[:, size:])
+
+                    out_out[...] = own_lanes(jnp.concatenate(
+                        [swap_out[part].reshape(2 * o_rows, 128) for part in range(out_count)], axis=1))
+                    qkv_out[...] = own_lanes(jnp.concatenate(
+                        [swap_qkv[part].reshape(2 * q_rows, 128) for part in range(q_parts)], axis=1))
                     for item in pieces:
                         item.close()
                     for copy in small_copies + late_copies:
@@ -701,19 +880,19 @@
     def number_of(g):
         return jnp.clip(g - 1, 0, attn_steps - 1)
 
-    def tile(which):
-        return pl.BlockSpec((length, 128), lambda g: (number_of(g) % docs, which * pairs + number_of(g) // docs))
+    tile = pl.BlockSpec((length, 128), lambda g: (number_of(g) % docs, number_of(g) // docs))
 
     two = (2,)
     any_space = pl.BlockSpec(memory_space=pl.ANY)
-    in_specs = [whole((rows, width)), whole((rows, width)), whole((width, width)), tile(0), tile(1), tile(2), tile(0)]
-    in_specs += [pl.BlockSpec((1, 1, length), lambda g: (number_of(g) % docs, 0, 0)), any_space]
-    in_specs += [any_space, any_space, whole((small_rows, width))]
+    in_specs = [any_space, any_space, any_space, tile, tile, tile]
+    in_specs += [pl.BlockSpec((1, 2, length, length), lambda g: (number_of(g) % docs, number_of(g) // docs, 0, 0))]
+    in_specs += [any_space, any_space, any_space, any_space, whole((small_rows, width))]
     out_shape = [
         jax.ShapeDtypeStruct((rows, width), jnp.bfloat16),
         jax.ShapeDtypeStruct((u_rows, ups * 128), jnp.float32),
-        jax.ShapeDtypeStruct((2, o_rows, lanes), jnp.float32),
-        jax.ShapeDtypeStruct((q_parts, 2, q_rows, 128), jnp.float32),
+        jax.ShapeDtypeStruct((2 * o_rows, lanes // 2), jnp.float32),
+        jax.ShapeDtypeStruct((2 * q_rows, lanes // 2), jnp.float32),
+        jax.ShapeDtypeStruct((d_rows, downs * 128), jnp.float32),
         jax.ShapeDtypeStruct((small_rows, width), jnp.float32),
         jax.ShapeDtypeStruct((8, 2 * width), jnp.float32),
     ]
@@ -723,28 +902,34 @@
         pltpu.VMEM((pairs, rows, 128), jnp.bfloat16),
         pltpu.VMEM((3 * width, rows), jnp.bfloat16),
         pltpu.VMEM(up_grads.shape, jnp.bfloat16),
-        pltpu.VMEM(wide_dims + half_dims + two + (o_rows, lanes), jnp.bfloat16),
+        pltpu.VMEM((out_count,) + wide_dims + half_dims + two + (o_rows, 128), jnp.bfloat16),
         pltpu.VMEM((q_parts,) + wide_dims + half_dims + two + (q_rows, 128), jnp.bfloat16),
     ]
-    scratch += [pltpu.VMEM((ups,) + two * (steps - 2 - s) + (u_rows, 128), jnp.bfloat16) for s in range(steps - 1)]
-    scratch += [pltpu.VMEM(two * (steps - 1 - s) + (o_rows, lanes), jnp.bfloat16) for s in range(steps)]
-    scratch += [pltpu.VMEM((q_parts,) + two * (steps - 1 - s) + (q_rows, 128), jnp.bfloat16) for s in range(steps)]
+    for low, high in u_cuts:
+        scratch += [pltpu.VMEM((ups,) + two * (steps - 2 - s) + (high - low, 128), jnp.bfloat16) for s in range(steps - 1)]
+    scratch += [pltpu.VMEM((out_count,) + two * (steps - 1 - s) + (o_rows, 128), jnp.bfloat16) for s in range(steps)]
+    for low, high in cuts:
+        scratch += [pltpu.VMEM((q_parts,) + two * (steps - 1 - s) + (high - low, 128), jnp.bfloat16) for s in range(steps)]
+    scratch += [pltpu.VMEM(down_grads.shape, jnp.bfloat16)]
+    scratch += [pltpu.VMEM((downs,) + two * (down_steps - 1 - s) + (d_rows, 128), jnp.bfloat16) for s in range(down_steps)]
     scratch += [pltpu.VMEM((steps, small_rows, width), jnp.float32)] * 2
     scratch += [pltpu.VMEM((steps, 8, 2 * width), jnp.float32)] * 2
-    scratch += [pltpu.VMEM(out_shape[2].shape, jnp.float32), pltpu.VMEM(out_shape[3].shape, jnp.float32)]
+    scratch += [pltpu.VMEM((out_count, 2, o_rows, 128), jnp.float32), pltpu.VMEM((q_parts, 2, q_rows, 128), jnp.float32)]
     scratch += [pltpu.VMEM(tokens.shape, jnp.bfloat16), pltpu.VMEM(qkv_weight.shape, jnp.bfloat16)]
-    sems = count * steps + 2 * steps + 1 + q_parts
-    scratch += [pltpu.SemaphoreType.DMA((sems,)), pltpu.SemaphoreType.DMA((sems,)), pltpu.SemaphoreType.DMA((ups + 2,))]
+    scratch += [pltpu.VMEM(item.shape, jnp.bfloat16) for item in (grad_attended, mixed, out_weight)]
+    sems = count * steps + 2 * steps + out_count + q_parts * len(cuts)
+    scratch += [pltpu.SemaphoreType.DMA((sems,)), pltpu.SemaphoreType.DMA((sems,)), pltpu.SemaphoreType.DMA((ups + 6,))]
     return pl.pallas_call(
         kernel,
         grid=(grid,),
         in_specs=in_specs,
-        out_specs=[whole(item.shape) for item in out_shape],
+        out_specs=[pl.BlockSpec((token_block, width), lambda g: (jnp.clip(g - first_t, 0, token_steps - 1), 0))]
+        + [whole(item.shape) for item in out_shape[1:]],
         out_shape=out_shape,
         scratch_shapes=scratch,
         compiler_params=pltpu.CompilerParams(collective_id=1, has_side_effects=True, vmem_limit_bytes=60 << 20),
         name="attention_backward",
-    )(grad_attended, mixed, out_weight, qkv, qkv, qkv, totals, key_bias, tokens, qkv_weight, up_grads, sums)
+    )(grad_attended, mixed, out_weight, queries, keys, values, attention, tokens, qkv_weight, up_grads, down_grads, sums)
 
 
 def on_device_fast(
@@ -772,63 +957,40 @@
     out_cotangent,
 ):
     doc_count, length, model_width = tokens.shape
-    low = jnp.bfloat16
     token_rows = tokens.reshape(doc_count * length, model_width)
-    allowed = lax.broadcasted_iota(jnp.int32, (doc_count, length), 1) < doc_lengths[:, None]
-    key_bias = jnp.where(allowed, 0.0, MASKED).astype(jnp.float32).reshape(doc_count, 1, length)
-    allowed_rows = allowed.reshape(-1, 1).astype(jnp.float32)
-    bias_row = jnp.concatenate([query_bias, jnp.zeros_like(query_bias), value_bias]).astype(jnp.float32)
-    qkv = (jnp.dot(token_rows, qkv_weight, preferred_element_type=jnp.float32) + bias_row).astype(low)
-    mixed, totals = attention_forward(qkv, key_bias, doc_count, length)
-    attended = jnp.dot(mixed, out_weight, preferred_element_type=jnp.float32) + out_bias.astype(jnp.float32)
-    resid_one = token_rows.astype(jnp.float32) + attended
-    hidden_one, normed_one, inverse_one = norm_forward(
-        resid_one, first_gain.astype(jnp.float32), first_shift.astype(jnp.float32)
-    )
-    hidden_low = hidden_one.astype(low)
-    upper_pre = jnp.dot(hidden_low, up_weight, preferred_element_type=jnp.float32) + up_bias.astype(jnp.float32)
-    cumulative = normal_cdf(upper_pre)
-    active = (upper_pre * cumulative).astype(low)
-    density = jnp.exp(-0.5 * upper_pre * upper_pre) * 0.3989422804014327
-    slope = (cumulative + upper_pre * density).astype(low)
-    lowered = jnp.dot(active, down_weight, preferred_element_type=jnp.float32) + down_bias.astype(jnp.float32)
-    resid_two = hidden_one + lowered
-    second_float = second_gain.astype(jnp.float32)
-    normed_out, normed_two, inverse_two = norm_forward(resid_two, second_float, second_shift.astype(jnp.float32))
-    encoded_rows = (normed_out * allowed_rows).astype(low)
+    rows_in = (out_bias, first_gain, first_shift, down_bias, second_gain, second_shift, query_bias, value_bias)
+    last = jnp.pad(dir_bias, (0, model_width - dir_bias.shape[0]))
+    vectors = jnp.concatenate([item[None] for item in rows_in + (last,)] + [up_bias.reshape(-1, model_width)])
+    vectors = vectors.astype(jnp.float32)
+    queries, keys, values, attention, mixed = attention_forward(doc_lengths, token_rows, qkv_weight, vectors)
+    hidden_low, normed_one, inverse_one, active, slope, normed_two, inverse_two, encoded_rows = ffn_forward(
+        doc_lengths, mixed, token_rows, out_weight, vectors, up_weight, down_weight
+    )
     classes_count = dir_weight.shape[1]
     doc_starts = lax.broadcasted_iota(jnp.int32, (doc_count, 1), 0) * length
     numbers = jnp.concatenate(
         [(segment_rows + doc_starts).reshape(1, -1), segment_slots, pair_rows[:, :, 0], pair_rows[:, :, 1], pair_labels]
-    )
-    numbers = jnp.pad(numbers, ((0, -numbers.shape[0] % 8), (0, 0)))
-    dir_rows = dir_weight.reshape(2, model_width, classes_count).transpose(0, 2, 1).reshape(-1, model_width)
-    grad_attended, up_blocks, out_down, sums = ffn_backward(
-        doc_lengths, numbers, encoded_rows, out_cotangent.reshape(-1, model_width), dir_rows,
-        dir_bias.astype(jnp.float32)[:, None], normed_two.astype(low), inverse_two, second_float[None], active, slope,
-        hidden_low, down_weight, up_weight, normed_one.astype(low), inverse_one, first_gain.astype(jnp.float32)[None],
-    )
-    grad_tokens, out_up, out_out, out_qkv, sums, late = attention_backward(
-        grad_attended, mixed, out_weight, qkv, totals, key_bias, token_rows, qkv_weight, up_blocks, sums
-    )
-    core = lax.axis_index("narrow") % 2
-    width = model_width // lax.axis_size("narrow")
-    out_qkv = out_qkv.transpose(1, 2, 0, 3).reshape(-1, 2 * width)
-    out_out = out_out.reshape(-1, 2 * width)
-
-    def own_lanes(rows):
-        return lax.dynamic_slice_in_dim(rows, core * width, width, 1).T
-
+        + [pair_labels] * 3
+    )
+    grad_attended, up_blocks, down_blocks, sums = ffn_backward(
+        doc_lengths, numbers, encoded_rows, out_cotangent.reshape(-1, model_width), dir_weight.T, vectors,
+        normed_two, inverse_two, active, slope,
+        hidden_low, down_weight, up_weight, normed_one, inverse_one,
+    )
+    grad_tokens, out_up, out_out, out_qkv, out_down, sums, late = attention_backward(
+        grad_attended, mixed, out_weight, queries, keys, values, attention, token_rows, qkv_weight, up_blocks,
+        down_blocks, sums,
+    )
     first_dir = 6 + lax.axis_size("narrow")
     last_dir = first_dir + 2 * classes_count
     dir_sum = sums[first_dir:last_dir].reshape(2, classes_count, model_width).transpose(0, 2, 1)
     return (
         encoded_rows.reshape(tokens.shape),
         grad_tokens.reshape(tokens.shape),
-        own_lanes(out_qkv),
+        out_qkv.T,
         late[0, :model_width],
         late[0, model_width:],
-        own_lanes(out_out),
+        out_out.T,
         sums[5],
         sums[3],
         sums[4],

time: 235 us -> 204 us (0.87)
  matrix products: 28.4 us -> 0 us
  local copies, waits for them, and re-layouts: 14.7 us -> 22.6 us
  Pallas kernels: 184 us -> 179 us
  other arithmetic: 5.89 us -> 1.38 us
    dot_general x4 -> x0, matrix products: 28.4 us -> none  [the longest x1 12.9 us: on_device_fast(): jnp.dot(hidden_low, up_weight, preferred_element_type=jnp.float32)]
    pallas_call x1, Pallas kernels: 78.2 us -> 56.7 us  [ffn_backward(): pl.pallas_call(kernel, grid=(2 * chunks,), in_specs=in_specs, out_specs=o...]
    pallas_call x2 -> x3, Pallas kernels: 106 us -> 122 us  [the longest x1 75.7 us: attention_backward(): pl.pallas_call(kernel, grid=(grid,), in_specs=in_specs, out_specs=[pl.Blo...]
    convert_element_type x10 -> x1, other arithmetic: 4.61 us -> 0.63 us  [on_device_fast(): vectors = vectors.astype(jnp.float32)]
    broadcast_in_dim x4 -> x9, local copies, waits for them, and re-layouts: 1.84 us -> 5.49 us  [on_device_fast(): item[None]]
    unnamed x65 -> x9, local copies, waits for them, and re-layouts: 5.03 us -> 7.61 us
where the time goes in v1:
time: 204 us
  Pallas kernels  179 us (88%)
  local copies, waits for them, and re-layouts  22.6 us (11%)
    pallas_call x1, Pallas kernels, attention_backward(): pl.pallas_call(kernel, grid=(grid,), in_specs=in_specs, out_specs=[pl.Blo...  75.7 us
    pallas_call x1, Pallas kernels, ffn_backward(): pl.pallas_call(kernel, grid=(2 * chunks,), in_specs=in_specs, out_specs=o...  56.7 us
    pallas_call x1, Pallas kernels, ffn_forward(): pl.pallas_call(kernel, grid=(chunks,), in_specs=[pl.BlockSpec(memory_spac...  25.5 us
    pallas_call x1, Pallas kernels, attention_forward(): pl.pallas_call(kernel, grid=(pairs,), in_specs=in_specs, out_specs=[colum...  21 us
    unnamed x9, local copies, waits for them, and re-layouts  7.61 us
    broadcast_in_dim x9, local copies, waits for them, and re-layouts, on_device_fast(): item[None]  5.49 us

profile of v1, /device:TPU:0, one launch (start us, length us, event | category | flops | bytes accessed | tf_op | source)
XLA Modules:
  0.0 203.6 jit_solution(10585108205368037870)
XLA Ops:
  0.7 0.8 broadcast_add_fusion
  2.1 0.8 slice_bitcast_fusion
  2.8 0.7 broadcast_in_dim.33
  3.5 0.7 broadcast_in_dim.34
  4.9 0.7 broadcast_in_dim.28
  5.6 0.7 broadcast_in_dim.29
  6.3 0.7 broadcast_in_dim.30
  7.0 0.7 broadcast_in_dim.31
  7.6 0.7 broadcast_in_dim.32
  8.3 1.4 concatenate.7.refs_1_
  9.8 0.7 reshape.67
  11.2 21.0 %attention_forward.1 = (bf16[1024,768]{1,0:T(8,128)(2,1)}, bf16[1024,768]{1,0:T(8,128)(2,1)}, bf16[1024,768]{1,0:T(8,128)(2,1)}, bf16[2,12,512,512]{3,2,1,0:T(8,128)(2,1)}, bf16[1024,768]{1,0:T(8,128)(2,1)}) custom-call(s32[2]{0:T(128)} %refs_0_.1, bf16[1024,768]{1,0:T(8,128)(2,1)} %bitcast.18, bf16[768,2304]{1,0:T(8,128)(2,1)} %refs_8_.1, ...), custom_call_target="tpu_custom_call" | custom-call | tf_op jit(solution)/shard_map/attention_forward/pallas_call | solution.py:174
  32.2 25.5 %ffn_forward.1 = (bf16[1024,768]{1,0:T(8,128)(2,1)}, bf16[1024,768]{1,0:T(8,128)(2,1)}, f32[1024,1]{1,0:T(8,128)}, bf16[1024,3072]{1,0:T(8,128)(2,1)}, bf16[1024...) custom-call(s32[2]{0:T(128)} %refs_0_.1, ...), custom_call_target="tpu_custom_call" | custom-call | tf_op jit(solution)/shard_map/ffn_forward/pallas_call | solution.py:250
  57.7 56.7 %ffn_backward.1 = (bf16[1024,768]{1,0:T(8,128)(2,1)}, bf16[3,2,2,2,2,192,128]{6,5,4,3,2,1,0:T(8,128)(2,1)}, bf16[6,2,2,96,128]{4,3,2,1,0:T(8,128)(2,1)}, f32[40,768]{1,0:T(8,128)}) custom-call(s32[2]{0:T(128)} %refs_0_.1, s32[8,256]{1,0:T(8,128)} %concatenate.7.refs_1_, bf16[1024,768]{1,0:T(8,128)(2,1)} %get-tuple-element.42.refs_2_, ...), custom_call_target="tpu_custom_call" | custom-call | tf_op jit(solution)/shard_map/ffn_backward/pallas_call | solution.py:588
  114.4 75.7 %attention_backward.1 = (bf16[1024,768]{1,0:T(8,128)(2,1)}, f32[192,384]{1,0:T(8,128)}, f32[96,192]{1,0:T(8,128)}, f32[288,192]{1,0:T(8,128)}, f32[96,768]{1,0:T...) custom-call(bf16[1024,768]{1,0:T(8,128)(2,1)} %get-tuple-element.50.refs_0_, ...), custom_call_target="tpu_custom_call" | custom-call | tf_op jit(solution)/shard_map/attention_backward/pallas_call | solution.py:922
  190.1 1.8 copy.41
  191.9 1.3 slice_reduce_fusion
  193.2 0.8 slice.46
  194.6 1.6 slice_reduce_fusion.1
  196.3 1.5 slice.50
  197.8 1.6 copy.42
  199.4 2.7 %copy.46 = bf16[2,512,768]{2,1,0:T(8,128)(2,1)} copy(bf16[2,512,768]{2,1,0:T(8,128)(2,1)} %bitcast.23) | data formatting | bytes 3145728
  202.1 0.7 copy.47
  202.9 0.7 copy.48
  (11 shorter events, 2.7 us)
Async XLA Ops:
  199.4 2.7 %copy-start.1 = (f32[192,384]{1,0:T(8,128)S(1)}, f32[192,384]{1,0:T(8,128)}, u32[]{:S(2)}) copy-start(f32[192,384]{1,0:T(8,128)} %get-tuple-element.137) | copy-start | bytes 884740
  199.4 3.4 %copy-start = (f32[96,768]{1,0:T(8,128)S(1)}, f32[96,768]{1,0:T(8,128)}, u32[]{:S(2)}) copy-start(f32[96,768]{1,0:T(8,128)} %get-tuple-element.64) | copy-start | bytes 884740

commit v2 on v1

--- a/solution.py
+++ b/solution.py
@@ -131,13 +131,28 @@
     return [core + narrow + x + near + far, core + x + near + narrow + far, core + near + narrow + x + far]
 
 
-def attention_forward(lengths, tokens, qkv_weight, vectors):
+def attention_forward(lengths, tokens, qkv_weight, singles):
     rows, width = tokens.shape
     docs = lengths.shape[0]
     length = rows // docs
     pairs = width // 128
 
-    def kernel(lens, tok, wq, wk, wv, vec, q_out, k_out, v_out, attention_out, mixed_out):
+    kinds = [item.shape[0] for item in singles]
+    lines = sum(max(1, size // width) for size in kinds)
+
+    def kernel(lens, tok, wq, wk, wv, *refs):
+        singles, (vec, q_out, k_out, v_out, attention_out, mixed_out) = refs[: len(kinds)], refs[len(kinds) :]
+
+        @pl.when(pl.program_id(0) == 0)
+        def _():
+            at = 0
+            for single, size in zip(singles, kinds):
+                values = single[...].astype(jnp.float32)
+                for first in range(0, size, width):
+                    some = min(size, width)
+                    vec[at, :some] = values[first : first + some]
+                    at += 1
+
         weights = jnp.concatenate([wq[...], wk[...], wv[...]], axis=1)
         at = pl.ds(pl.multiple_of(pl.program_id(0) * 128, 128), 128)
         offsets = jnp.concatenate([vec[6:7, at], jnp.zeros((1, 128), jnp.float32), vec[7:8, at]], axis=1)
@@ -169,18 +184,18 @@
     column = pl.BlockSpec((rows, 128), lambda pair: (0, pair))
     in_specs = [pl.BlockSpec(memory_space=pltpu.SMEM), whole((rows, width))]
     in_specs += [pl.BlockSpec((width, 128), lambda pair, n=n: (0, n * pairs + pair)) for n in range(3)]
-    in_specs += [whole(vectors.shape)]
+    in_specs += [whole(item.shape) for item in singles]
     low = jax.ShapeDtypeStruct((rows, width), jnp.bfloat16)
     return pl.pallas_call(
         kernel,
         grid=(pairs,),
         in_specs=in_specs,
-        out_specs=[column] * 3
+        out_specs=[whole((lines, width))] + [column] * 3
         + [pl.BlockSpec((docs, 2, length, length), lambda pair: (0, pair, 0, 0)), column],
-        out_shape=[low] * 3 + [jax.ShapeDtypeStruct((docs, 2 * pairs, length, length), jnp.bfloat16), low],
+        out_shape=[jax.ShapeDtypeStruct((lines, width), jnp.float32)] + [low] * 3 + [jax.ShapeDtypeStruct((docs, 2 * pairs, length, length), jnp.bfloat16), low],
         compiler_params=pltpu.CompilerParams(vmem_limit_bytes=56 << 20),
         name="attention_forward",
-    )(lengths, tokens, qkv_weight, qkv_weight, qkv_weight, vectors)
+    )(lengths, tokens, qkv_weight, qkv_weight, qkv_weight, *singles)
 
 
 def ffn_forward(lengths, mixed, tokens, out_weight, vectors, up_weight, down_weight):
@@ -189,7 +204,7 @@
     chunk = width
     chunks = ff // chunk
     length = rows // lengths.shape[0]
-    row_block = 128
+    row_block = 256
 
     def kernel(lens, mix, tok, ow, vec, up, down, hid_out, n1_out, q1_out, act_out, slope_out, n2_out, q2_out,
                enc_out, hidden, total):
@@ -288,11 +303,12 @@
     return jnp.where(lines == row, 1.0, 0.0).astype(jnp.bfloat16)
 
 
-def ffn_backward(lengths, numbers, encoded, cotangent, dir_t, vectors, normed_two, inverse_two, active, slope, hidden_low, down_weight, up_weight,
+def ffn_backward(lengths, segment_rows, segment_slots, pair_rows, pair_labels, encoded, cotangent, dir_t, vectors, normed_two, inverse_two, active, slope, hidden_low, down_weight, up_weight,
                  normed_one, inverse_one):
     rows, width = hidden_low.shape
     ff = active.shape[1]
-    segments, classes = numbers.shape[1], dir_t.shape[0]
+    segments, classes = segment_slots.shape[1], dir_t.shape[0]
+    numbers = (segment_rows, segment_slots, pair_rows, pair_labels)
     length = rows // lengths.shape[0]
     names = axis_bits()
     steps = len(names)
@@ -301,7 +317,7 @@
     chunks = ff // narrow // 128
     third = chunks // 2
     d_rows, u_rows = width // wide, width // narrow
-    row_block = 128
+    row_block = 256
     row_steps = rows // row_block
     orders = link_orders()
     two = (2,)
@@ -317,8 +333,8 @@
         return tuple((number >> bit) & 1 for bit in reversed(range(count)))
 
     def kernel(*refs):
-        lens, nums, enc, cot, dir_ref = refs[:5]
-        refs = refs[5:]
+        lens, seg_rows, seg_slots, pair_nums, labels, enc, cot, dir_ref = refs[:8]
+        refs = refs[8:]
         q2, q1, vec = refs[:3]
         far = refs[3:9]
         slo = refs[9 : 9 + narrow]
@@ -357,7 +373,7 @@
                 local_sems.at[number],
             )
 
-        def exchange(source, landing, first):
+        def exchange(source, landing, first, meanwhile=None):
             made = []
             for offset in range(1, wide):
                 target = place.ahead(offset)
@@ -369,9 +385,20 @@
             for copy in made:
                 copy.start()
             landing[me] = source[me]
+            if meanwhile:
+                meanwhile()
             for copy in made:
                 copy.wait()
             return landing[...].reshape(segments, 128)
+
+        def turn_hidden():
+            def body(i, carry):
+                some = pl.ds(pl.multiple_of(i * row_block, row_block), row_block)
+                hidden_t[:, some] = hidden[some, :].T
+                return carry
+
+            loads[1].wait()
+            lax.fori_loop(0, row_steps, body, 0)
 
         @pl.when(pid == 0)
         def _():
@@ -380,14 +407,16 @@
             place.greet(all_wide=True)
             sums_out[...] = jnp.zeros_like(sums_out)
             base = chunks * early + chunks
-            select[...] = dot_last(one_hot(nums[0:1, :], rows), one_hot(nums[1:2, :], segments)).astype(jnp.bfloat16)
+            docs = rows // length
+            places = jnp.concatenate([seg_rows[doc : doc + 1, :] + doc * length for doc in range(docs)], axis=1)
+            select[...] = dot_last(one_hot(places, rows), one_hot(seg_slots[...], segments)).astype(jnp.bfloat16)
             picked[...] = jnp.dot(select[...].T, enc[...], preferred_element_type=jnp.float32).astype(jnp.bfloat16)
             halves = [dir_ref[:, n * width : (n + 1) * width].astype(jnp.float32) for n in range(2)]
             blank = jnp.zeros((128 - 2 * classes, width), jnp.float32)
             dir_w[...] = jnp.concatenate(halves + [blank]).astype(jnp.bfloat16)
             leaving[...] = dot_last(picked[...], dir_w[...]).reshape(leaving.shape)
-            scores = exchange(leaving, arrived, base).T
-            pair_first, pair_second = one_hot(nums[2:3, :], segments), one_hot(nums[3:4, :], segments)
+            scores = exchange(leaving, arrived, base, turn_hidden).T
+            pair_first, pair_second = one_hot(pair_nums[0:1, :], segments), one_hot(pair_nums[1:2, :], segments)
 
             def chosen(values, pairs):
                 split = jnp.dot(parts_of(values, 3), pairs, preferred_element_type=jnp.float32)
@@ -398,7 +427,7 @@
             powers = jnp.exp(logits - jnp.max(logits, 0, keepdims=True))
             chance = powers / jnp.sum(powers, 0, keepdims=True)
             kinds = lax.broadcasted_iota(jnp.int32, logits.shape, 0)
-            delta = chance - jnp.where(kinds == nums[4:5, :], 1.0, 0.0)
+            delta = chance - jnp.where(kinds == labels[...], 1.0, 0.0)
             split = parts_of(delta, 2)
             gathered = []
             for pairs in (pair_first, pair_second):
@@ -420,7 +449,6 @@
             both = jnp.dot(parts_of(back_t, 2), picked[...], preferred_element_type=jnp.float32)
             sums_out[first_dir : first_dir + 2 * classes, :] = both[: 2 * classes] + both[2 * classes :]
             loads[0].wait()
-            loads[1].wait()
 
             def body(i, carry):
                 at = pl.multiple_of(i * row_block, row_block)
@@ -437,7 +465,6 @@
                 grad_hidden[some, :] = two
                 lowered[some, :] = low
                 lowered_t[:, some] = low.T
-                hidden_t[:, some] = hidden[some, :].T
                 sums_out[0:1, :] += jnp.sum(grad * normed, 0, keepdims=True)
                 sums_out[1:2, :] += jnp.sum(grad, 0, keepdims=True)
                 sums_out[2:3, :] += jnp.sum(low.astype(jnp.float32), 0, keepdims=True)
@@ -549,7 +576,8 @@
     def slab_columns(shape, first):
         return [pl.BlockSpec(shape, lambda g, n=n: (0, n * chunks + chunk_of(g - first))) for n in range(narrow)]
 
-    in_specs = [pl.BlockSpec(memory_space=pltpu.SMEM), whole(numbers.shape), whole((rows, width)), whole((rows, width))]
+    in_specs = [pl.BlockSpec(memory_space=pltpu.SMEM), *[whole(item.shape) for item in numbers],
+                whole((rows, width)), whole((rows, width))]
     in_specs += [whole(dir_t.shape)]
     in_specs += [whole((rows, 1))] * 2 + [whole(vectors.shape)] + [pl.BlockSpec(memory_space=pl.ANY)] * 6
     in_specs += slab_columns((rows, 128), chunks)
@@ -594,7 +622,7 @@
         scratch_shapes=scratch,
         compiler_params=pltpu.CompilerParams(collective_id=0, has_side_effects=True, vmem_limit_bytes=60 << 20),
         name="ffn_backward",
-    )(lengths, numbers, encoded, cotangent, dir_t, inverse_two, inverse_one, vectors,
+    )(lengths, *numbers, encoded, cotangent, dir_t, inverse_two, inverse_one, vectors,
       *far, *([slope] * narrow))
 
 
@@ -932,6 +960,50 @@
     )(grad_attended, mixed, out_weight, queries, keys, values, attention, tokens, qkv_weight, up_grads, down_grads, sums)
 
 
+def hand_out(grad_tokens, sums, late, narrow, classes, turned, *blocks):
+    rows, width = grad_tokens.shape
+    steps = 4
+    first_dir = 6 + narrow
+
+    def kernel(tokens_ref, sums_ref, late_ref, *refs):
+        ins, outs = refs[: len(blocks)], refs[len(blocks) :]
+        outs[0][...] = tokens_ref[...]
+
+        @pl.when(pl.program_id(0) == 0)
+        def _():
+            for source, target in zip(ins, outs[1:]):
+                target[...] = source[...] if source.shape == target.shape else source[...].T
+            singles = outs[1 + len(blocks) :]
+            for number in range(6):
+                singles[number][...] = sums_ref[number, :]
+            for number in range(2):
+                singles[6 + number][...] = late_ref[0, number * width : (number + 1) * width]
+            for number in range(narrow):
+                singles[8][number * width : (number + 1) * width] = sums_ref[6 + number, :]
+            singles[9][...] = sums_ref[first_dir : first_dir + 2 * classes, :]
+            square = (classes, 128)
+            matching = lax.broadcasted_iota(jnp.int32, square, 0) == lax.broadcasted_iota(jnp.int32, square, 1)
+            biases = sums_ref[first_dir + 2 * classes : first_dir + 3 * classes, :128]
+            singles[10][...] = jnp.sum(jnp.where(matching, biases, 0.0), 0)[:classes]
+
+    def whole(shape):
+        return pl.BlockSpec(shape, lambda g: (0,) * len(shape))
+
+    some = pl.BlockSpec((rows // steps, width), lambda g: (g, 0))
+    small = [(width,)] * 8 + [(narrow * width,), (2 * classes, width), (classes,)]
+    shapes = [block.shape[::-1] if number in turned else block.shape for number, block in enumerate(blocks)]
+    out_shape = [jax.ShapeDtypeStruct((rows, width), jnp.bfloat16)]
+    out_shape += [jax.ShapeDtypeStruct(shape, jnp.float32) for shape in shapes + small]
+    return pl.pallas_call(
+        kernel,
+        grid=(steps,),
+        in_specs=[some] + [whole(item.shape) for item in (sums, late) + blocks],
+        out_specs=[some] + [whole(item.shape) for item in out_shape[1:]],
+        out_shape=out_shape,
+        name="hand_out",
+    )(grad_tokens, sums, late, *blocks)
+
+
 def on_device_fast(
     tokens,
     doc_lengths,
@@ -958,22 +1030,16 @@
 ):
     doc_count, length, model_width = tokens.shape
     token_rows = tokens.reshape(doc_count * length, model_width)
-    rows_in = (out_bias, first_gain, first_shift, down_bias, second_gain, second_shift, query_bias, value_bias)
-    last = jnp.pad(dir_bias, (0, model_width - dir_bias.shape[0]))
-    vectors = jnp.concatenate([item[None] for item in rows_in + (last,)] + [up_bias.reshape(-1, model_width)])
-    vectors = vectors.astype(jnp.float32)
-    queries, keys, values, attention, mixed = attention_forward(doc_lengths, token_rows, qkv_weight, vectors)
+    singles = (out_bias, first_gain, first_shift, down_bias, second_gain, second_shift, query_bias, value_bias)
+    vectors, queries, keys, values, attention, mixed = attention_forward(
+        doc_lengths, token_rows, qkv_weight, singles + (dir_bias, up_bias)
+    )
     hidden_low, normed_one, inverse_one, active, slope, normed_two, inverse_two, encoded_rows = ffn_forward(
         doc_lengths, mixed, token_rows, out_weight, vectors, up_weight, down_weight
     )
     classes_count = dir_weight.shape[1]
-    doc_starts = lax.broadcasted_iota(jnp.int32, (doc_count, 1), 0) * length
-    numbers = jnp.concatenate(
-        [(segment_rows + doc_starts).reshape(1, -1), segment_slots, pair_rows[:, :, 0], pair_rows[:, :, 1], pair_labels]
-        + [pair_labels] * 3
-    )
     grad_attended, up_blocks, down_blocks, sums = ffn_backward(
-        doc_lengths, numbers, encoded_rows, out_cotangent.reshape(-1, model_width), dir_weight.T, vectors,
+        doc_lengths, segment_rows, segment_slots, pair_rows[0].T, pair_labels, encoded_rows, out_cotangent.reshape(-1, model_width), dir_weight.T, vectors,
         normed_two, inverse_two, active, slope,
         hidden_low, down_weight, up_weight, normed_one, inverse_one,
     )
@@ -981,27 +1047,27 @@
         grad_attended, mixed, out_weight, queries, keys, values, attention, token_rows, qkv_weight, up_blocks,
         down_blocks, sums,
     )
-    first_dir = 6 + lax.axis_size("narrow")
-    last_dir = first_dir + 2 * classes_count
-    dir_sum = sums[first_dir:last_dir].reshape(2, classes_count, model_width).transpose(0, 2, 1)
+    grad_tokens, out_up, out_out, out_qkv, out_down, *smalls = hand_out(
+        grad_tokens, sums, late, lax.axis_size("narrow"), classes_count, (1, 2), out_up, out_out, out_qkv, out_down
+    )
     return (
         encoded_rows.reshape(tokens.shape),
         grad_tokens.reshape(tokens.shape),
-        out_qkv.T,
-        late[0, :model_width],
-        late[0, model_width:],
-        out_out.T,
-        sums[5],
-        sums[3],
-        sums[4],
+        out_qkv,
+        smalls[6],
+        smalls[7],
+        out_out,
+        smalls[5],
+        smalls[3],
+        smalls[4],
         out_up,
-        sums[6:first_dir].reshape(-1),
+        smalls[8],
         out_down.T,
-        sums[2],
-        sums[0],
-        sums[1],
-        dir_sum.reshape(2 * model_width, classes_count),
-        sums[last_dir : last_dir + classes_count, 0],
+        smalls[2],
+        smalls[0],
+        smalls[1],
+        smalls[9].reshape(2, classes_count, model_width).transpose(0, 2, 1).reshape(2 * model_width, classes_count),
+        smalls[10],
     )
 
 

time: 204 us -> 182 us (0.89)
  local copies, waits for them, and re-layouts: 22.6 us -> 0 us
    unnamed x9 -> x0, local copies, waits for them, and re-layouts: 7.61 us -> none
    broadcast_in_dim x9 -> x0, local copies, waits for them, and re-layouts: 5.49 us -> none  [on_device_fast(): item[None]]
    slice x4 -> x0, local copies, waits for them, and re-layouts: 5.27 us -> none  [the longest x1 1.64 us: on_device_fast(): sums[1]]
    pallas_call x1 -> x2, Pallas kernels: 21 us -> 25.9 us  [the longest x1 21.3 us: attention_forward(): pl.pallas_call(kernel, grid=(pairs,), in_specs=in_specs, out_specs=[whole...]
where the time goes in v2:
time: 182 us
  Pallas kernels  181 us (99%)
    pallas_call x1, Pallas kernels, attention_backward(): pl.pallas_call(kernel, grid=(grid,), in_specs=in_specs, out_specs=[pl.Blo...  75.6 us
    pallas_call x1, Pallas kernels, ffn_backward(): pl.pallas_call(kernel, grid=(2 * chunks,), in_specs=in_specs, out_specs=o...  55.4 us
    pallas_call x1, Pallas kernels, ffn_forward(): pl.pallas_call(kernel, grid=(chunks,), in_specs=[pl.BlockSpec(memory_spac...  24.2 us
    pallas_call x1, Pallas kernels, attention_forward(): pl.pallas_call(kernel, grid=(pairs,), in_specs=in_specs, out_specs=[whole...  21.3 us
    pallas_call x1, Pallas kernels, hand_out(): pl.pallas_call(kernel, grid=(steps,), in_specs=[some] + [whole(item.shape...  4.58 us

profile of v2, /device:TPU:0, one launch (start us, length us, event | category | flops | bytes accessed | tf_op | source)
XLA Modules:
  0.0 182.0 jit_solution(7731970888482547293)
XLA Ops:
  0.7 21.3 %attention_forward.1 = (f32[13,768]{1,0:T(8,128)}, bf16[1024,768]{1,0:T(8,128)(2,1)}, bf16[1024,768]{1,0:T(8,128)(2,1)}, bf16[1024,768]{1,0:T(8,128)(2,1)}, bf16...) custom-call(s32[2]{0:T(128)} %refs_0_.3, bf16[1024,768]{1,0:T(8,128)(2,1)} %bitcast.14, ...), custom_call_target="tpu_custom_call" | custom-call | tf_op jit(solution)/shard_map/attention_forward/pallas_call | solution.py:189
  22.0 24.2 %ffn_forward.1 = (bf16[1024,768]{1,0:T(8,128)(2,1)}, bf16[1024,768]{1,0:T(8,128)(2,1)}, f32[1024,1]{1,0:T(8,128)}, bf16[1024,3072]{1,0:T(8,128)(2,1)}, bf16[1024...) custom-call(s32[2]{0:T(128)} %refs_0_.3, ...), custom_call_target="tpu_custom_call" | custom-call | tf_op jit(solution)/shard_map/ffn_forward/pallas_call | solution.py:265
  46.3 55.4 %ffn_backward.1 = (bf16[1024,768]{1,0:T(8,128)(2,1)}, bf16[3,2,2,2,2,192,128]{6,5,4,3,2,1,0:T(8,128)(2,1)}, bf16[6,2,2,96,128]{4,3,2,1,0:T(8,128)(2,1)}, f32[40,768]{1,0:T(8,128)}) custom-call(s32[2]{0:T(128)} %refs_0_.3, s32[2,128]{1,0:T(2,128)} %refs_1_.3, s32[1,256]{1,0:T(1,128)} %refs_2_.4, s32[2,256]{1,0:T(2,128)} %bitcast.20, s32[1,256]{1,0:T(1,128)} %refs_4_.3, ...), custom_call_target="tpu_custom_call" | custom-call | tf_op jit(solution)/shard_map/ffn_backward/pallas_call | solution.py:616
  101.6 75.6 %attention_backward.1 = (bf16[1024,768]{1,0:T(8,128)(2,1)}, f32[192,384]{1,0:T(8,128)}, f32[96,192]{1,0:T(8,128)}, f32[288,192]{1,0:T(8,128)}, f32[96,768]{1,0:T...) custom-call(bf16[1024,768]{1,0:T(8,128)(2,1)} %get-tuple-element.68.refs_0_, ...), custom_call_target="tpu_custom_call" | custom-call | tf_op jit(solution)/shard_map/attention_backward/pallas_call | solution.py:950
  177.3 4.6 %hand_out.1 = (bf16[1024,768]{1,0:T(8,128)(2,1)}, f32[192,384]{1,0:T(8,128)}, f32[192,96]{1,0:T(8,128)}, f32[192,288]{1,0:T(8,128)}, f32[96,768]{1,0:T(8,128)}, ...) custom-call(bf16[1024,768]{1,0:T(8,128)(2,1)} %get-tuple-element.76., ...), custom_call_target="tpu_custom_call" | custom-call | tf_op jit(solution)/shard_map/hand_out/pallas_call | solution.py:997

commit v3 on v2

--- a/solution.py
+++ b/solution.py
@@ -323,7 +323,7 @@
     two = (2,)
     early = 3
     first_dir = 6 + narrow
-    sum_rows = pl.cdiv(first_dir + 3 * classes, 8) * 8
+    sum_rows = pl.cdiv(first_dir + 2 * classes + 1, 16) * 16
 
     def chunk_of(step):
         step = jnp.clip(step, 0, chunks - 1)
@@ -435,9 +435,10 @@
                 gathered.append(both[:classes] + both[classes:])
             gathered.append(jnp.zeros((128 - 2 * classes, segments), jnp.float32))
             leaving_grads[...] = jnp.concatenate(gathered).T.reshape(leaving.shape)
-            sums_out[first_dir + 2 * classes : first_dir + 3 * classes, :] = jnp.broadcast_to(
-                jnp.sum(delta, 1, keepdims=True), (classes, width)
-            )
+            square = (classes, 128)
+            matching = lax.broadcasted_iota(jnp.int32, square, 0) == lax.broadcasted_iota(jnp.int32, square, 1)
+            biases = jnp.where(matching, jnp.sum(delta, 1, keepdims=True), 0.0)
+            sums_out[first_dir + 2 * classes : first_dir + 2 * classes + 1, :128] = jnp.sum(biases, 0, keepdims=True)
             back = exchange(leaving_grads, arrived_grads, base + wide - 1)
             coarse = back.astype(jnp.bfloat16)
             fine = (back - coarse.astype(jnp.float32)).astype(jnp.bfloat16)
@@ -658,6 +659,8 @@
     first_down = first_part + q_parts * len(cuts)
     count = first_down + downs
     small_rows = sums.shape[0]
+    late_rows = pl.cdiv(2 * pairs, 8) * 8
+    s_cuts = [(0, small_rows // 4), (small_rows // 4, small_rows // 2), (small_rows // 2, small_rows)]
 
     def bits_of(number, count):
         return tuple((number >> bit) & 1 for bit in reversed(range(count)))
@@ -700,17 +703,20 @@
                                   len(pieces) * steps))
         base = count * steps
 
-        def all_sum(sent, received, first):
+        def all_sum(sent, received, first, order=0, rows=slice(None)):
             made = []
             for step in range(steps):
                 made.append(pltpu.make_async_remote_copy(
-                    src_ref=sent.at[step], dst_ref=received.at[step], send_sem=send_sems.at[first + step],
-                    recv_sem=recv_sems.at[first + step], device_id=place.across(orders[0][step]),
+                    src_ref=sent.at[step, rows], dst_ref=received.at[step, rows], send_sem=send_sems.at[first + step],
+                    recv_sem=recv_sems.at[first + step], device_id=place.across(orders[order][step]),
                     device_id_type=MESH_ID))
             return made
 
-        small_copies = all_sum(small_sent, small_received, base)
-        late_copies = all_sum(late_sent, late_received, base + steps)
+        small_copies = [
+            all_sum(small_sent, small_received, base + (2 + q_parts * len(cuts) + i) * steps + out_count, i, slice(low, high))
+            for i, (low, high) in enumerate(s_cuts)
+        ]
+        late_copies = [all_sum(late_sent, late_received, base + steps)]
         swap_refs = [swap_out.at[part, core] for part in range(out_count)]
         swap_refs += [swap_qkv.at[part, core, low:high] for part in range(q_parts) for low, high in cuts]
         swaps = [pltpu.make_async_remote_copy(
@@ -750,12 +756,14 @@
                     swap_qkv[part, core, cuts[cut][0] : cuts[cut][1]] = total
                 swaps[number - up_count].start()
 
-        def advance_small(copies, sent, received, out, step):
-            copies[step].wait_recv()
+        def advance_small(lanes, sent, received, out, step):
+            for copies in lanes:
+                copies[step].wait_recv()
             total = sent[step] + received[step]
             if step + 1 < steps:
                 sent[step + 1] = total
-                copies[step + 1].start()
+                for copies in lanes:
+                    copies[step + 1].start()
             else:
                 out[...] = total
 
@@ -769,7 +777,8 @@
             for load in first_loads:
                 load.start()
             small_sent[0] = small[...]
-            small_copies[0].start()
+            for copies in small_copies:
+                copies[0].start()
             down_load.start()
             for load in loads:
                 load.start()
@@ -831,10 +840,14 @@
                     for load in loads:
                         load.wait()
                     ones = jnp.ones((8, rows), jnp.bfloat16)
-                    late_sent[0] = jnp.concatenate(
-                        [dot_last(ones, gqkv_t[:width, :]), dot_last(ones, gqkv_t[2 * width :, :])], axis=1
-                    )
-                    late_copies[0].start()
+                    for which in range(2):
+                        totals = dot_last(ones, gqkv_t[2 * which * width : (2 * which + 1) * width, :])
+                        for j in range(pairs):
+                            late_sent[0, which * pairs + j : which * pairs + j + 1, :] = totals[
+                                :1, j * 128 : (j + 1) * 128
+                            ]
+                    late_sent[0, 2 * pairs :, :] = jnp.zeros((late_rows - 2 * pairs, 128), jnp.float32)
+                    late_copies[0][0].start()
                 columns = jnp.concatenate(
                     [tok[:, y * lanes + part * 128 : y * lanes + (part + 1) * 128] for y in range(half)], axis=1
                 )
@@ -857,21 +870,21 @@
             tokens_out[...] = (grad_t.T + ga[some, :].astype(jnp.float32)).astype(jnp.bfloat16)
 
         plan, small_plan, late_plan = {}, {}, {}
-        for cut, times in enumerate(((4, 7, 9, 12), (6, 8, 10, 14))):
+        for cut, times in enumerate(((5, 9, 12, 14), (8, 10, 13, 15))):
             for step, at in enumerate(times):
                 for part in range(ups):
                     plan.setdefault(at, []).append((cut * ups + part, step))
-        for step, at in enumerate((1, 8, 10, 12, 14)):
+        for step, at in enumerate((1, 9, 12, 14, 15)):
             for part in range(out_count):
                 plan.setdefault(at, []).append((up_count + part, step))
-        for step, at in enumerate((3, 6)):
+        for step, at in enumerate((4, 8)):
             for number in range(downs):
                 plan.setdefault(at, []).append((first_down + number, step))
         for number in range(first_part, first_down):
             for step in range(steps):
                 at = first_q + (number - first_part) // len(cuts) + 1 if step == 0 else grid - 1
                 plan.setdefault(at, []).append((number, step))
-        for step, at in enumerate((3, 6, 8, 10, 12)):
+        for step, at in enumerate((3, 7, 9, 11, 13)):
             small_plan[at] = step
         late_plan[first_q + 2] = 0
         for at in range(grid):
@@ -899,8 +912,9 @@
                         [swap_qkv[part].reshape(2 * q_rows, 128) for part in range(q_parts)], axis=1))
                     for item in pieces:
                         item.close()
-                    for copy in small_copies + late_copies:
-                        copy.wait_send()
+                    for copies in small_copies + late_copies:
+                        for copy in copies:
+                            copy.wait_send()
 
     def whole(shape):
         return pl.BlockSpec(shape, lambda g: (0,) * len(shape), pipeline_mode=pl.Buffered(1))
@@ -922,7 +936,7 @@
         jax.ShapeDtypeStruct((2 * q_rows, lanes // 2), jnp.float32),
         jax.ShapeDtypeStruct((d_rows, downs * 128), jnp.float32),
         jax.ShapeDtypeStruct((small_rows, width), jnp.float32),
-        jax.ShapeDtypeStruct((8, 2 * width), jnp.float32),
+        jax.ShapeDtypeStruct((late_rows, 128), jnp.float32),
     ]
     wide_dims, half_dims = two * wide_bits, two * half_bits
     scratch = [
@@ -941,11 +955,11 @@
     scratch += [pltpu.VMEM(down_grads.shape, jnp.bfloat16)]
     scratch += [pltpu.VMEM((downs,) + two * (down_steps - 1 - s) + (d_rows, 128), jnp.bfloat16) for s in range(down_steps)]
     scratch += [pltpu.VMEM((steps, small_rows, width), jnp.float32)] * 2
-    scratch += [pltpu.VMEM((steps, 8, 2 * width), jnp.float32)] * 2
+    scratch += [pltpu.VMEM((steps, late_rows, 128), jnp.float32)] * 2
     scratch += [pltpu.VMEM((out_count, 2, o_rows, 128), jnp.float32), pltpu.VMEM((q_parts, 2, q_rows, 128), jnp.float32)]
     scratch += [pltpu.VMEM(tokens.shape, jnp.bfloat16), pltpu.VMEM(qkv_weight.shape, jnp.bfloat16)]
     scratch += [pltpu.VMEM(item.shape, jnp.bfloat16) for item in (grad_attended, mixed, out_weight)]
-    sems = count * steps + 2 * steps + out_count + q_parts * len(cuts)
+    sems = count * steps + (2 + q_parts * len(cuts) + len(s_cuts)) * steps + out_count
     scratch += [pltpu.SemaphoreType.DMA((sems,)), pltpu.SemaphoreType.DMA((sems,)), pltpu.SemaphoreType.DMA((ups + 6,))]
     return pl.pallas_call(
         kernel,
@@ -977,14 +991,12 @@
             for number in range(6):
                 singles[number][...] = sums_ref[number, :]
             for number in range(2):
-                singles[6 + number][...] = late_ref[0, number * width : (number + 1) * width]
+                for j in range(width // 128):
+                    singles[6 + number][j * 128 : (j + 1) * 128] = late_ref[number * (width // 128) + j, :]
             for number in range(narrow):
                 singles[8][number * width : (number + 1) * width] = sums_ref[6 + number, :]
             singles[9][...] = sums_ref[first_dir : first_dir + 2 * classes, :]
-            square = (classes, 128)
-            matching = lax.broadcasted_iota(jnp.int32, square, 0) == lax.broadcasted_iota(jnp.int32, square, 1)
-            biases = sums_ref[first_dir + 2 * classes : first_dir + 3 * classes, :128]
-            singles[10][...] = jnp.sum(jnp.where(matching, biases, 0.0), 0)[:classes]
+            singles[10][...] = sums_ref[first_dir + 2 * classes, :classes]
 
     def whole(shape):
         return pl.BlockSpec(shape, lambda g: (0,) * len(shape))

time: 182 us -> 175 us (0.962)
  Pallas kernels: 181 us -> 174 us
    pallas_call x1, Pallas kernels: 75.6 us -> 68.4 us  [attention_backward(): pl.pallas_call(kernel, grid=(grid,), in_specs=in_specs, out_specs=[pl.Blo...]
where the time goes in v3:
time: 175 us
  Pallas kernels  174 us (99%)
    pallas_call x1, Pallas kernels, attention_backward(): pl.pallas_call(kernel, grid=(grid,), in_specs=in_specs, out_specs=[pl.Blo...  68.4 us
    pallas_call x1, Pallas kernels, ffn_backward(): pl.pallas_call(kernel, grid=(2 * chunks,), in_specs=in_specs, out_specs=o...  55.4 us
    pallas_call x1, Pallas kernels, ffn_forward(): pl.pallas_call(kernel, grid=(chunks,), in_specs=[pl.BlockSpec(memory_spac...  24.2 us
    pallas_call x1, Pallas kernels, attention_forward(): pl.pallas_call(kernel, grid=(pairs,), in_specs=in_specs, out_specs=[whole...  21.3 us
    pallas_call x1, Pallas kernels, hand_out(): pl.pallas_call(kernel, grid=(steps,), in_specs=[some] + [whole(item.shape...  4.59 us

profile of v3, /device:TPU:0, one launch (start us, length us, event | category | flops | bytes accessed | tf_op | source)
XLA Modules:
  0.0 174.8 jit_solution(10112224161708231110)
XLA Ops:
  0.7 21.3 %attention_forward.1 = (f32[13,768]{1,0:T(8,128)}, bf16[1024,768]{1,0:T(8,128)(2,1)}, bf16[1024,768]{1,0:T(8,128)(2,1)}, bf16[1024,768]{1,0:T(8,128)(2,1)}, bf16...) custom-call(s32[2]{0:T(128)} %refs_0_.3, bf16[1024,768]{1,0:T(8,128)(2,1)} %bitcast.14, ...), custom_call_target="tpu_custom_call" | custom-call | tf_op jit(solution)/shard_map/attention_forward/pallas_call | solution.py:189
  22.0 24.2 %ffn_forward.1 = (bf16[1024,768]{1,0:T(8,128)(2,1)}, bf16[1024,768]{1,0:T(8,128)(2,1)}, f32[1024,1]{1,0:T(8,128)}, bf16[1024,3072]{1,0:T(8,128)(2,1)}, bf16[1024...) custom-call(s32[2]{0:T(128)} %refs_0_.3, ...), custom_call_target="tpu_custom_call" | custom-call | tf_op jit(solution)/shard_map/ffn_forward/pallas_call | solution.py:265
  46.3 55.4 %ffn_backward.1 = (bf16[1024,768]{1,0:T(8,128)(2,1)}, bf16[3,2,2,2,2,192,128]{6,5,4,3,2,1,0:T(8,128)(2,1)}, bf16[6,2,2,96,128]{4,3,2,1,0:T(8,128)(2,1)}, f32[32,768]{1,0:T(8,128)}) custom-call(s32[2]{0:T(128)} %refs_0_.3, s32[2,128]{1,0:T(2,128)} %refs_1_.3, s32[1,256]{1,0:T(1,128)} %refs_2_.4, s32[2,256]{1,0:T(2,128)} %bitcast.20, s32[1,256]{1,0:T(1,128)} %refs_4_.3, ...), custom_call_target="tpu_custom_call" | custom-call | tf_op jit(solution)/shard_map/ffn_backward/pallas_call | solution.py:617
  101.7 68.4 %attention_backward.1 = (bf16[1024,768]{1,0:T(8,128)(2,1)}, f32[192,384]{1,0:T(8,128)}, f32[96,192]{1,0:T(8,128)}, f32[288,192]{1,0:T(8,128)}, f32[96,768]{1,0:T...) custom-call(bf16[1024,768]{1,0:T(8,128)(2,1)} %get-tuple-element.68.refs_0_, ...), custom_call_target="tpu_custom_call" | custom-call | tf_op jit(solution)/shard_map/attention_backward/pallas_call | solution.py:964
  170.1 4.6 %hand_out.1 = (bf16[1024,768]{1,0:T(8,128)(2,1)}, f32[192,384]{1,0:T(8,128)}, f32[192,96]{1,0:T(8,128)}, f32[192,288]{1,0:T(8,128)}, f32[96,768]{1,0:T(8,128)}, ...) custom-call(bf16[1024,768]{1,0:T(8,128)(2,1)} %get-tuple-element.76., ...), custom_call_target="tpu_custom_call" | custom-call | tf_op jit(solution)/shard_map/hand_out/pallas_call | solution.py:1009

commit v4 on v3

--- a/solution.py
+++ b/solution.py
@@ -131,19 +131,31 @@
     return [core + narrow + x + near + far, core + x + near + narrow + far, core + near + narrow + x + far]
 
 
-def attention_forward(lengths, tokens, qkv_weight, singles):
+def layer_forward(lengths, tokens, qkv_weight, out_weight, up_weight, down_weight, singles):
     rows, width = tokens.shape
+    ff = up_weight.shape[1]
     docs = lengths.shape[0]
     length = rows // docs
-    pairs = width // 128
-
+    pairs, chunks = width // 128, ff // width
     kinds = [item.shape[0] for item in singles]
     lines = sum(max(1, size // width) for size in kinds)
-
-    def kernel(lens, tok, wq, wk, wv, *refs):
-        singles, (vec, q_out, k_out, v_out, attention_out, mixed_out) = refs[: len(kinds)], refs[len(kinds) :]
-
-        @pl.when(pl.program_id(0) == 0)
+    row_block = 256
+
+    def kernel(lens, tok, wq, wk, wv, ow, up, down, *refs):
+        singles, refs = refs[: len(kinds)], refs[len(kinds) :]
+        vec, q_out, k_out, v_out, attention_out, mixed_out = refs[:6]
+        hid_out, n1_out, q1_out, act_out, slope_out, n2_out, q2_out, enc_out = refs[6:14]
+        mixed, hidden, total = refs[14:]
+        pid = pl.program_id(0)
+
+        def each_block(body):
+            def step(i, carry):
+                body(pl.multiple_of(i * row_block, row_block))
+                return carry
+
+            lax.fori_loop(0, rows // row_block, step, 0)
+
+        @pl.when(pid == 0)
         def _():
             at = 0
             for single, size in zip(singles, kinds):
@@ -153,73 +165,38 @@
                     vec[at, :some] = values[first : first + some]
                     at += 1
 
-        weights = jnp.concatenate([wq[...], wk[...], wv[...]], axis=1)
-        at = pl.ds(pl.multiple_of(pl.program_id(0) * 128, 128), 128)
-        offsets = jnp.concatenate([vec[6:7, at], jnp.zeros((1, 128), jnp.float32), vec[7:8, at]], axis=1)
-        qkv = (jnp.dot(tok[...], weights, preferred_element_type=jnp.float32) + offsets).astype(jnp.bfloat16)
-        q_out[...] = qkv[:, :128]
-        k_out[...] = qkv[:, 128:256]
-        v_out[...] = qkv[:, 256:]
-        first = lax.broadcasted_iota(jnp.int32, (1, 128), 1) < HEAD_DIM
-        for doc in range(docs):
-            some = slice(doc * length, (doc + 1) * length)
-            queries = qkv[some, :128] * jnp.bfloat16(HEAD_DIM**-0.5)
-            keys, values = qkv[some, 128:256], qkv[some, 256:]
-            zero = jnp.zeros_like(queries)
-            places = lax.broadcasted_iota(jnp.int32, (1, length), 1)
-            bias = jnp.where(places < lens[doc], 0.0, MASKED)
-            outs = []
-            for head in range(2):
-                masked = jnp.where(first, queries, zero) if head == 0 else jnp.where(first, zero, queries)
-                scores = dot_last(masked, keys) + bias
-                powers = jnp.exp(scores - jnp.max(scores, -1, keepdims=True))
-                attention = (powers * (1.0 / jnp.sum(powers, -1, keepdims=True))).astype(jnp.bfloat16)
-                attention_out[doc, head] = attention
-                outs.append(jnp.dot(attention, values, preferred_element_type=jnp.float32))
-            mixed_out[some, :] = jnp.where(first, outs[0], outs[1]).astype(jnp.bfloat16)
-
-    def whole(shape):
-        return pl.BlockSpec(shape, lambda pair: (0,) * len(shape), pipeline_mode=pl.Buffered(1))
-
-    column = pl.BlockSpec((rows, 128), lambda pair: (0, pair))
-    in_specs = [pl.BlockSpec(memory_space=pltpu.SMEM), whole((rows, width))]
-    in_specs += [pl.BlockSpec((width, 128), lambda pair, n=n: (0, n * pairs + pair)) for n in range(3)]
-    in_specs += [whole(item.shape) for item in singles]
-    low = jax.ShapeDtypeStruct((rows, width), jnp.bfloat16)
-    return pl.pallas_call(
-        kernel,
-        grid=(pairs,),
-        in_specs=in_specs,
-        out_specs=[whole((lines, width))] + [column] * 3
-        + [pl.BlockSpec((docs, 2, length, length), lambda pair: (0, pair, 0, 0)), column],
-        out_shape=[jax.ShapeDtypeStruct((lines, width), jnp.float32)] + [low] * 3 + [jax.ShapeDtypeStruct((docs, 2 * pairs, length, length), jnp.bfloat16), low],
-        compiler_params=pltpu.CompilerParams(vmem_limit_bytes=56 << 20),
-        name="attention_forward",
-    )(lengths, tokens, qkv_weight, qkv_weight, qkv_weight, *singles)
-
-
-def ffn_forward(lengths, mixed, tokens, out_weight, vectors, up_weight, down_weight):
-    rows, width = tokens.shape
-    ff = up_weight.shape[1]
-    chunk = width
-    chunks = ff // chunk
-    length = rows // lengths.shape[0]
-    row_block = 256
-
-    def kernel(lens, mix, tok, ow, vec, up, down, hid_out, n1_out, q1_out, act_out, slope_out, n2_out, q2_out,
-               enc_out, hidden, total):
-        pid = pl.program_id(0)
-
-        def each_block(body):
-            def step(i, carry):
-                body(pl.multiple_of(i * row_block, row_block))
-                return carry
-
-            lax.fori_loop(0, rows // row_block, step, 0)
-
-        @pl.when(pid == 0)
+        @pl.when(pid < pairs)
         def _():
-            total[...] = jnp.dot(mix[...], ow[...], preferred_element_type=jnp.float32)
+            weights = jnp.concatenate([wq[...], wk[...], wv[...]], axis=1)
+            at = pl.ds(pl.multiple_of(pid * 128, 128), 128)
+            offsets = jnp.concatenate([vec[6:7, at], jnp.zeros((1, 128), jnp.float32), vec[7:8, at]], axis=1)
+            qkv = (jnp.dot(tok[...], weights, preferred_element_type=jnp.float32) + offsets).astype(jnp.bfloat16)
+            q_out[...] = qkv[:, :128]
+            k_out[...] = qkv[:, 128:256]
+            v_out[...] = qkv[:, 256:]
+            first = lax.broadcasted_iota(jnp.int32, (1, 128), 1) < HEAD_DIM
+            for doc in range(docs):
+                some = slice(doc * length, (doc + 1) * length)
+                queries = qkv[some, :128] * jnp.bfloat16(HEAD_DIM**-0.5)
+                keys, values = qkv[some, 128:256], qkv[some, 256:]
+                zero = jnp.zeros_like(queries)
+                places = lax.broadcasted_iota(jnp.int32, (1, length), 1)
+                bias = jnp.where(places < lens[doc], 0.0, MASKED)
+                outs = []
+                for head in range(2):
+                    masked = jnp.where(first, queries, zero) if head == 0 else jnp.where(first, zero, queries)
+                    scores = dot_last(masked, keys) + bias
+                    powers = jnp.exp(scores - jnp.max(scores, -1, keepdims=True))
+                    attention = (powers * (1.0 / jnp.sum(powers, -1, keepdims=True))).astype(jnp.bfloat16)
+                    attention_out[doc, head] = attention
+                    outs.append(jnp.dot(attention, values, preferred_element_type=jnp.float32))
+                both = jnp.where(first, outs[0], outs[1]).astype(jnp.bfloat16)
+                mixed_out[some, :] = both
+                mixed[some, at] = both
+
+        @pl.when(pid == pairs)
+        def _():
+            total[...] = jnp.dot(mixed[...], ow[...], preferred_element_type=jnp.float32)
 
             def body(at):
                 some = pl.ds(at, row_block)
@@ -233,15 +210,18 @@
 
             each_block(body)
 
-        pre = jnp.dot(hid_out[...], up[...], preferred_element_type=jnp.float32) + vec[pl.ds(pid + 9, 1), :]
-        cumulative = normal_cdf(pre)
-        density = jnp.exp(-0.5 * pre * pre) * 0.3989422804014327
-        active = (pre * cumulative).astype(jnp.bfloat16)
-        act_out[...] = active
-        slope_out[...] = (cumulative + pre * density).astype(jnp.bfloat16)
-        total[...] += jnp.dot(active, down[...], preferred_element_type=jnp.float32)
-
-        @pl.when(pid == chunks - 1)
+        @pl.when(pid >= pairs)
+        def _():
+            offset = vec[pl.ds(pid - pairs + 9, 1), :]
+            pre = jnp.dot(hid_out[...], up[...], preferred_element_type=jnp.float32) + offset
+            cumulative = normal_cdf(pre)
+            density = jnp.exp(-0.5 * pre * pre) * 0.3989422804014327
+            active = (pre * cumulative).astype(jnp.bfloat16)
+            act_out[...] = active
+            slope_out[...] = (cumulative + pre * density).astype(jnp.bfloat16)
+            total[...] += jnp.dot(active, down[...], preferred_element_type=jnp.float32)
+
+        @pl.when(pid == pairs + chunks - 1)
         def _():
             def body(at):
                 some = pl.ds(at, row_block)
@@ -256,26 +236,39 @@
             each_block(body)
 
     def whole(shape):
-        return pl.BlockSpec(shape, lambda f: (0,) * len(shape), pipeline_mode=pl.Buffered(1))
-
-    wide_row, column = whole((rows, width)), pl.BlockSpec((rows, chunk), lambda f: (0, f))
+        return pl.BlockSpec(shape, lambda g: (0,) * len(shape), pipeline_mode=pl.Buffered(1))
+
+    def pair_of(g):
+        return jnp.minimum(g, pairs - 1)
+
+    def chunk_of(g):
+        return jnp.clip(g - pairs, 0, chunks - 1)
+
+    column = pl.BlockSpec((rows, 128), lambda g: (0, pair_of(g)))
+    upper = pl.BlockSpec((rows, width), lambda g: (0, chunk_of(g)))
+    full, one = whole((rows, width)), whole((rows, 1))
+    in_specs = [pl.BlockSpec(memory_space=pltpu.SMEM), full]
+    in_specs += [pl.BlockSpec((width, 128), lambda g, n=n: (0, n * pairs + pair_of(g))) for n in range(3)]
+    in_specs += [whole((width, width)), pl.BlockSpec((width, width), lambda g: (0, chunk_of(g)))]
+    in_specs += [pl.BlockSpec((width, width), lambda g: (chunk_of(g), 0))]
+    in_specs += [whole(item.shape) for item in singles]
     low = jax.ShapeDtypeStruct((rows, width), jnp.bfloat16)
-    one = jax.ShapeDtypeStruct((rows, 1), jnp.float32)
-    upper = jax.ShapeDtypeStruct((rows, ff), jnp.bfloat16)
+    inverse = jax.ShapeDtypeStruct((rows, 1), jnp.float32)
+    high = jax.ShapeDtypeStruct((rows, ff), jnp.bfloat16)
     return pl.pallas_call(
         kernel,
-        grid=(chunks,),
-        in_specs=[
-            pl.BlockSpec(memory_space=pltpu.SMEM), wide_row, wide_row, whole((width, width)), whole(vectors.shape),
-            pl.BlockSpec((width, chunk), lambda f: (0, f)),
-            pl.BlockSpec((chunk, width), lambda f: (f, 0)),
-        ],
-        out_specs=[wide_row, wide_row, whole((rows, 1)), column, column, wide_row, whole((rows, 1)), wide_row],
-        out_shape=[low, low, one, upper, upper, low, one, low],
-        scratch_shapes=[pltpu.VMEM((rows, width), jnp.float32), pltpu.VMEM((rows, width), jnp.float32)],
-        compiler_params=pltpu.CompilerParams(vmem_limit_bytes=58 << 20),
-        name="ffn_forward",
-    )(lengths, mixed, tokens, out_weight, vectors, up_weight, down_weight)
+        grid=(pairs + chunks,),
+        in_specs=in_specs,
+        out_specs=[whole((lines, width))] + [column] * 3
+        + [pl.BlockSpec((docs, 2, length, length), lambda g: (0, pair_of(g), 0, 0)), column]
+        + [full, full, one, upper, upper, full, one, full],
+        out_shape=[jax.ShapeDtypeStruct((lines, width), jnp.float32)] + [low] * 3
+        + [jax.ShapeDtypeStruct((docs, 2 * pairs, length, length), jnp.bfloat16), low]
+        + [low, low, inverse, high, high, low, inverse, low],
+        scratch_shapes=[pltpu.VMEM((rows, width), jnp.bfloat16)] + [pltpu.VMEM((rows, width), jnp.float32)] * 2,
+        compiler_params=pltpu.CompilerParams(vmem_limit_bytes=60 << 20),
+        name="layer_forward",
+    )(lengths, tokens, qkv_weight, qkv_weight, qkv_weight, out_weight, up_weight, down_weight, *singles)
 
 
 def dot_last(left, right):
@@ -550,7 +543,7 @@
         plan = {}
         for number in range(chunks):
             for step in range(early):
-                at = (number + 1, chunks + 1 + 2 * (number // 3), chunks + 4 + number // 3)[step]
+                at = (number + 2, chunks + 1 + 2 * (number // 3), chunks + 4 + number // 3)[step]
                 plan.setdefault(min(at, 2 * chunks - 1), []).append((step, number))
         for at in range(2 * chunks):
             @pl.when(pid == at)
@@ -1043,12 +1036,10 @@
     doc_count, length, model_width = tokens.shape
     token_rows = tokens.reshape(doc_count * length, model_width)
     singles = (out_bias, first_gain, first_shift, down_bias, second_gain, second_shift, query_bias, value_bias)
-    vectors, queries, keys, values, attention, mixed = attention_forward(
-        doc_lengths, token_rows, qkv_weight, singles + (dir_bias, up_bias)
-    )
-    hidden_low, normed_one, inverse_one, active, slope, normed_two, inverse_two, encoded_rows = ffn_forward(
-        doc_lengths, mixed, token_rows, out_weight, vectors, up_weight, down_weight
-    )
+    vectors, queries, keys, values, attention, mixed, *kept = layer_forward(
+        doc_lengths, token_rows, qkv_weight, out_weight, up_weight, down_weight, singles + (dir_bias, up_bias)
+    )
+    hidden_low, normed_one, inverse_one, active, slope, normed_two, inverse_two, encoded_rows = kept
     classes_count = dir_weight.shape[1]
     grad_attended, up_blocks, down_blocks, sums = ffn_backward(
         doc_lengths, segment_rows, segment_slots, pair_rows[0].T, pair_labels, encoded_rows, out_cotangent.reshape(-1, model_width), dir_weight.T, vectors,

time: 175 us -> 172 us (0.983)
  Pallas kernels: 174 us -> 171 us
    pallas_call x2 -> x1, Pallas kernels: 45.6 us -> 44.3 us  [layer_forward(): pl.pallas_call(kernel, grid=(pairs + chunks,), in_specs=in_specs, out_spe...]
where the time goes in v4:
time: 172 us
  Pallas kernels  171 us (99%)
    pallas_call x1, Pallas kernels, attention_backward(): pl.pallas_call(kernel, grid=(grid,), in_specs=in_specs, out_specs=[pl.Blo...  67 us
    pallas_call x1, Pallas kernels, ffn_backward(): pl.pallas_call(kernel, grid=(2 * chunks,), in_specs=in_specs, out_specs=o...  55.2 us
    pallas_call x1, Pallas kernels, layer_forward(): pl.pallas_call(kernel, grid=(pairs + chunks,), in_specs=in_specs, out_spe...  44.3 us
    pallas_call x1, Pallas kernels, hand_out(): pl.pallas_call(kernel, grid=(steps,), in_specs=[some] + [whole(item.shape...  4.59 us

profile of v4, /device:TPU:0, one launch (start us, length us, event | category | flops | bytes accessed | tf_op | source)
XLA Modules:
  0.0 171.9 jit_solution(173892877048555561)
XLA Ops:
  0.7 44.3 %layer_forward.1 = (f32[13,768]{1,0:T(8,128)}, bf16[1024,768]{1,0:T(8,128)(2,1)}, bf16[1024,768]{1,0:T(8,128)(2,1)}, bf16[1024,768]{1,0:T(8,128)(2,1)}, bf16[2,1...) custom-call(s32[2]{0:T(128)} %refs_0_.3, ...), custom_call_target="tpu_custom_call" | custom-call | tf_op jit(solution)/shard_map/layer_forward/pallas_call | solution.py:258
  44.9 55.2 %ffn_backward.1 = (bf16[1024,768]{1,0:T(8,128)(2,1)}, bf16[3,2,2,2,2,192,128]{6,5,4,3,2,1,0:T(8,128)(2,1)}, bf16[6,2,2,96,128]{4,3,2,1,0:T(8,128)(2,1)}, f32[32,768]{1,0:T(8,128)}) custom-call(s32[2]{0:T(128)} %refs_0_.3, s32[2,128]{1,0:T(2,128)} %refs_1_.3, s32[1,256]{1,0:T(1,128)} %refs_2_.4, s32[2,256]{1,0:T(2,128)} %bitcast.19, s32[1,256]{1,0:T(1,128)} %refs_4_.3, ...), custom_call_target="tpu_custom_call" | custom-call | tf_op jit(solution)/shard_map/ffn_backward/pallas_call | solution.py:610
  100.1 67.0 %attention_backward.1 = (bf16[1024,768]{1,0:T(8,128)(2,1)}, f32[192,384]{1,0:T(8,128)}, f32[96,192]{1,0:T(8,128)}, f32[288,192]{1,0:T(8,128)}, f32[96,768]{1,0:T...) custom-call(bf16[1024,768]{1,0:T(8,128)(2,1)} %get-tuple-element.67.refs_0_, bf16[1024,768]{1,0:T(8,128)(2,1)} %get-tuple-element.68.refs_1_, ...), custom_call_target="tpu_custom_call" | custom-call | tf_op jit(solution)/shard_map/attention_backward/pallas_call | solution.py:957
  167.1 4.6 %hand_out.1 = (bf16[1024,768]{1,0:T(8,128)(2,1)}, f32[192,384]{1,0:T(8,128)}, f32[192,96]{1,0:T(8,128)}, f32[192,288]{1,0:T(8,128)}, f32[96,768]{1,0:T(8,128)}, ...) custom-call(bf16[1024,768]{1,0:T(8,128)(2,1)} %get-tuple-element.76., ...), custom_call_target="tpu_custom_call" | custom-call | tf_op jit(solution)/shard_map/hand_out/pallas_call | solution.py:1002

commit v5 on v4

--- a/solution.py
+++ b/solution.py
@@ -969,7 +969,7 @@
 
 def hand_out(grad_tokens, sums, late, narrow, classes, turned, *blocks):
     rows, width = grad_tokens.shape
-    steps = 4
+    steps = 2
     first_dir = 6 + narrow
 
     def kernel(tokens_ref, sums_ref, late_ref, *refs):

time: 172 us -> 171 us (level)
  no operation moved by 1% of the time
where the time goes in v5:
time: 171 us
  Pallas kernels  170 us (99%)
    pallas_call x1, Pallas kernels, attention_backward(): pl.pallas_call(kernel, grid=(grid,), in_specs=in_specs, out_specs=[pl.Blo...  67 us
    pallas_call x1, Pallas kernels, ffn_backward(): pl.pallas_call(kernel, grid=(2 * chunks,), in_specs=in_specs, out_specs=o...  55.2 us
    pallas_call x1, Pallas kernels, layer_forward(): pl.pallas_call(kernel, grid=(pairs + chunks,), in_specs=in_specs, out_spe...  44.3 us

profile of v5, /device:TPU:0, one launch (start us, length us, event | category | flops | bytes accessed | tf_op | source)
XLA Modules:
  0.0 170.6 jit_solution(16663733938156083534)
XLA Ops:
  0.7 44.3 %layer_forward.1 = (f32[13,768]{1,0:T(8,128)}, bf16[1024,768]{1,0:T(8,128)(2,1)}, bf16[1024,768]{1,0:T(8,128)(2,1)}, bf16[1024,768]{1,0:T(8,128)(2,1)}, bf16[2,1...) custom-call(s32[2]{0:T(128)} %refs_0_.3, ...), custom_call_target="tpu_custom_call" | custom-call | tf_op jit(solution)/shard_map/layer_forward/pallas_call | solution.py:258
  44.9 55.2 %ffn_backward.1 = (bf16[1024,768]{1,0:T(8,128)(2,1)}, bf16[3,2,2,2,2,192,128]{6,5,4,3,2,1,0:T(8,128)(2,1)}, bf16[6,2,2,96,128]{4,3,2,1,0:T(8,128)(2,1)}, f32[32,768]{1,0:T(8,128)}) custom-call(s32[2]{0:T(128)} %refs_0_.3, s32[2,128]{1,0:T(2,128)} %refs_1_.3, s32[1,256]{1,0:T(1,128)} %refs_2_.4, s32[2,256]{1,0:T(2,128)} %bitcast.19, s32[1,256]{1,0:T(1,128)} %refs_4_.3, ...), custom_call_target="tpu_custom_call" | custom-call | tf_op jit(solution)/shard_map/ffn_backward/pallas_call | solution.py:610
  100.1 67.0 %attention_backward.1 = (bf16[1024,768]{1,0:T(8,128)(2,1)}, f32[192,384]{1,0:T(8,128)}, f32[96,192]{1,0:T(8,128)}, f32[288,192]{1,0:T(8,128)}, f32[96,768]{1,0:T...) custom-call(bf16[1024,768]{1,0:T(8,128)(2,1)} %get-tuple-element.67.refs_0_, bf16[1024,768]{1,0:T(8,128)(2,1)} %get-tuple-element.68.refs_1_, ...), custom_call_target="tpu_custom_call" | custom-call | tf_op jit(solution)/shard_map/attention_backward/pallas_call | solution.py:957
  167.1 3.3 %hand_out.1 = (bf16[1024,768]{1,0:T(8,128)(2,1)}, f32[192,384]{1,0:T(8,128)}, f32[192,96]{1,0:T(8,128)}, f32[192,288]{1,0:T(8,128)}, f32[96,768]{1,0:T(8,128)}, ...) custom-call(bf16[1024,768]{1,0:T(8,128)(2,1)} %get-tuple-element.76., ...), custom_call_target="tpu_custom_call" | custom-call | tf_op jit(solution)/shard_map/hand_out/pallas_call | solution.py:1002

commit v6 on v5

--- a/solution.py
+++ b/solution.py
@@ -139,7 +139,7 @@
     pairs, chunks = width // 128, ff // width
     kinds = [item.shape[0] for item in singles]
     lines = sum(max(1, size // width) for size in kinds)
-    row_block = 256
+    row_block = 512
 
     def kernel(lens, tok, wq, wk, wv, ow, up, down, *refs):
         singles, refs = refs[: len(kinds)], refs[len(kinds) :]
@@ -310,7 +310,7 @@
     chunks = ff // narrow // 128
     third = chunks // 2
     d_rows, u_rows = width // wide, width // narrow
-    row_block = 256
+    row_block = 512
     row_steps = rows // row_block
     orders = link_orders()
     two = (2,)
@@ -645,7 +645,7 @@
     grid = first_t + token_steps
     downs, d_rows = down_grads.shape[0], down_grads.shape[-2]
     down_steps = len(down_grads.shape) - 3
-    cuts = [(0, q_rows // 32 * 16), (q_rows // 32 * 16, q_rows)]
+    cuts = [(0, q_rows // 24 * 16), (q_rows // 24 * 16, q_rows)]
     u_cuts = [(0, u_rows // 2), (u_rows // 2, u_rows)]
     up_count, out_count = ups * len(u_cuts), q_parts
     first_part = up_count + out_count
@@ -880,12 +880,16 @@
         for step, at in enumerate((3, 7, 9, 11, 13)):
             small_plan[at] = step
         late_plan[first_q + 2] = 0
+        def turn(at, number, step):
+            cut = (number - first_part) % len(cuts) if first_part <= number < first_down and at == grid - 1 else 0
+            return step + cut, step, number
+
         for at in range(grid):
             @pl.when(pid == at)
             def _():
                 if at in small_plan:
                     advance_small(small_copies, small_sent, small_received, small_out, small_plan[at])
-                for number, step in sorted(plan.get(at, []), key=lambda entry: (entry[1], entry[0])):
+                for number, step in sorted(plan.get(at, []), key=lambda entry: turn(at, *entry)):
                     if at == grid - 1 and number == first_part:
                         advance_small(late_copies, late_sent, late_received, late_out, step)
                     advance(number, step)

time: 171 us -> 170 us (level)
  no operation moved by 1% of the time
where the time goes in v6:
time: 170 us
  Pallas kernels  169 us (99%)
    pallas_call x1, Pallas kernels, attention_backward(): pl.pallas_call(kernel, grid=(grid,), in_specs=in_specs, out_specs=[pl.Blo...  66.6 us
    pallas_call x1, Pallas kernels, ffn_backward(): pl.pallas_call(kernel, grid=(2 * chunks,), in_specs=in_specs, out_specs=o...  54.7 us
    pallas_call x1, Pallas kernels, layer_forward(): pl.pallas_call(kernel, grid=(pairs + chunks,), in_specs=in_specs, out_spe...  44.3 us

profile of v6, /device:TPU:0, one launch (start us, length us, event | category | flops | bytes accessed | tf_op | source)
XLA Modules:
  0.0 169.8 jit_solution(17142652943992831601)
XLA Ops:
  0.7 44.3 %layer_forward.1 = (f32[13,768]{1,0:T(8,128)}, bf16[1024,768]{1,0:T(8,128)(2,1)}, bf16[1024,768]{1,0:T(8,128)(2,1)}, bf16[1024,768]{1,0:T(8,128)(2,1)}, bf16[2,1...) custom-call(s32[2]{0:T(128)} %refs_0_.3, ...), custom_call_target="tpu_custom_call" | custom-call | tf_op jit(solution)/shard_map/layer_forward/pallas_call | solution.py:258
  45.0 54.7 %ffn_backward.1 = (bf16[1024,768]{1,0:T(8,128)(2,1)}, bf16[3,2,2,2,2,192,128]{6,5,4,3,2,1,0:T(8,128)(2,1)}, bf16[6,2,2,96,128]{4,3,2,1,0:T(8,128)(2,1)}, f32[32,768]{1,0:T(8,128)}) custom-call(s32[2]{0:T(128)} %refs_0_.3, s32[2,128]{1,0:T(2,128)} %refs_1_.3, s32[1,256]{1,0:T(1,128)} %refs_2_.4, s32[2,256]{1,0:T(2,128)} %bitcast.19, s32[1,256]{1,0:T(1,128)} %refs_4_.3, ...), custom_call_target="tpu_custom_call" | custom-call | tf_op jit(solution)/shard_map/ffn_backward/pallas_call | solution.py:610
  99.8 66.6 %attention_backward.1 = (bf16[1024,768]{1,0:T(8,128)(2,1)}, f32[192,384]{1,0:T(8,128)}, f32[96,192]{1,0:T(8,128)}, f32[288,192]{1,0:T(8,128)}, f32[96,768]{1,0:T...) custom-call(bf16[1024,768]{1,0:T(8,128)(2,1)} %get-tuple-element.67.refs_0_, bf16[1024,768]{1,0:T(8,128)(2,1)} %get-tuple-element.68.refs_1_, ...), custom_call_target="tpu_custom_call" | custom-call | tf_op jit(solution)/shard_map/attention_backward/pallas_call | solution.py:961
  166.4 3.3 %hand_out.1 = (bf16[1024,768]{1,0:T(8,128)(2,1)}, f32[192,384]{1,0:T(8,128)}, f32[192,96]{1,0:T(8,128)}, f32[192,288]{1,0:T(8,128)}, f32[96,768]{1,0:T(8,128)}, ...) custom-call(bf16[1024,768]{1,0:T(8,128)(2,1)} %get-tuple-element.76., ...), custom_call_target="tpu_custom_call" | custom-call | tf_op jit(solution)/shard_map/hand_out/pallas_call | solution.py:1006
